TPU v7x, 128 devices: a whole 4x4x4 slice. The times are simulated.
128 devices in a mesh: radar: 8 (over x, core), tile: 16 (over y, z).
Axes of the slice: x: 4, y: 4, z: 4, core: 2. Of those that a mesh axis runs over, the one named last changes fastest.
Arguments:
- background: float32 [3, 256, 32, 2048], P(None, 'tile', None, 'radar'), may hold values from -6 to 6
- interp: bfloat16 [32768, 128, 128], P(('radar', 'tile')), may hold values from -0.5 to 0.5
- beam: bfloat16 [32768, 3, 128], P(('radar', 'tile')), may hold values from -1 to 1
- observed: bfloat16 [32768, 128], P(('radar', 'tile')), may hold values from -6 to 6
- cell_block: int32 [32768], P(('radar', 'tile')), may hold values from 0 to 1023
- sweep_count: int32 [128, 128], P(('radar', 'tile')), may hold values from 0 to 2, as said below
Outputs:
- wind_field: float32 [3, 256, 32, 2048], P(None, 'tile', None, 'radar')
- strain: float32 [6, 256, 32, 2048], P(None, 'tile', None, 'radar')
- cost_trace: float32 [2], replicated
Inputs may be any that keep to these rules, and one draw needn't show every extreme that they name: `cell_block`: the cell block, within the owner's 16 x 32 x 256 cells of one component, read by a slot. `sweep_count`: every source device has an owning device to which all 2 of its slots are live.
All inputs are finite; a program needn't handle non-finite values.
Results may differ from a plain program's by a relative error of at most 0.0014.
Values may be sent and summed in bfloat16 or wider, within the bound.
A program may use at most 64 MiB of HBM per device.

v0:
```python
import jax
import jax.numpy as jnp
from jax import lax
from jax.sharding import Mesh
from jax.sharding import PartitionSpec as P

ITERS = 2
RADAR_TILE = ("radar_0", "radar_1", "tile_0", "tile_1")
RADAR = ("radar_0", "radar_1")
TILE = ("tile_0", "tile_1")


BACKGROUND_WEIGHT = 0.5
DIVERGENCE_WEIGHT = 1.0
STEP_LENGTH = 0.3
EPSILON = 1e-06


def padded_2(x, sides, width):
    edges = {}
    for axis, dim in sides:
        size, length = (lax.axis_size(axis), x.shape[dim])
        up = [(i, (i + 1) % size) for i in range(size - 1)]
        last = lax.slice_in_dim(x, length - width, length, axis=dim)
        first = lax.slice_in_dim(x, 0, width, axis=dim)
        edges[dim] = (
            lax.ppermute(last, axis, up),
            lax.ppermute(first, axis, [(b, a) for a, b in up]),
        )
    done = []
    for _, dim in sides:
        low, high = edges[dim]
        around = [(width, width) if d in done else (0, 0) for d in range(x.ndim)]
        x = jnp.concatenate([jnp.pad(low, around), x, jnp.pad(high, around)], axis=dim)
        done.append(dim)
    return x


def split_up(x, dim, length):
    before, after = (x.shape[:dim], x.shape[dim + 1 :])
    return jnp.moveaxis(x.reshape(*before, length, -1, *after), dim, 0)


def laid_out(tiles, dim):
    tiles = jnp.moveaxis(tiles, 0, dim)
    shape = tiles.shape
    return tiles.reshape(*shape[:dim], shape[dim] * shape[dim + 1], *shape[dim + 2 :])


def joined_exchange(x, axis, axes, splits, concats):
    sizes = [lax.axis_size(a) for a in axes]
    tiles = split_up(x, splits[0], sizes[0])
    tiles = jnp.moveaxis(split_up(tiles, splits[1] + 1, sizes[1]), 0, 1)
    inside = tiles.shape[2:]
    tiles = tiles.reshape(-1, *inside)
    tiles = lax.all_to_all(tiles, axis, split_axis=0, concat_axis=0, tiled=True)
    tiles = laid_out(tiles.reshape(*sizes, *inside), concats[0] + 1)
    return laid_out(tiles, concats[1])


def over_axes(x, axes):
    for axis in axes:
        x = lax.psum(x, axis)
    return x


def vertical_diff(values):
    padded = jnp.pad(values, ((0, 0), (1, 1), (0, 0)))
    return 0.5 * (padded[:, 2:, :] - padded[:, :-2, :])


def along_x(values):
    return 0.5 * (values[2:, :, 1:-1] - values[:-2, :, 1:-1])


def along_y(values):
    return 0.5 * (values[1:-1, :, 2:] - values[1:-1, :, :-2])


def along_z(values):
    return vertical_diff(values[1:-1, :, 1:-1])


def observe(cell_rows, weights, beam_rows, looked, alive_mask):
    projected = jnp.einsum("knc,ngc->nkg", cell_rows, weights, preferred_element_type=jnp.float32)
    beam_values = beam_rows.astype(jnp.float32)
    radial = jnp.sum(beam_values * projected, axis=1)
    misfit = alive_mask[:, None] * (radial - looked.astype(jnp.float32))
    adjoint = (beam_values * misfit[:, None, :]).astype(jnp.bfloat16)
    returned = jnp.einsum("nkg,ngc->knc", adjoint, weights, preferred_element_type=jnp.float32)
    return (0.5 * jnp.sum(misfit * misfit), returned)


def spread_faces(wind_field):
    faces = padded_2(wind_field[:2], ((RADAR, 3), (TILE, 1)), 1)
    spread = along_x(faces[0]) + along_y(faces[1]) + vertical_diff(wind_field[2])
    beside_all = padded_2(spread, ((RADAR, 2), (TILE, 0)), 1)
    push = jnp.stack([-along_x(beside_all), -along_y(beside_all), -vertical_diff(spread)])
    return (spread, push)


def shards(background, interp, beam, observed, cell_block, sweep_count):
    radar_count = lax.axis_size(RADAR)
    tile_count = lax.axis_size(TILE)
    devices = radar_count * tile_count
    width_x = background.shape[1]
    levels = background.shape[2]
    width_y = background.shape[3]
    slots = interp.shape[0] // devices
    gate_size = interp.shape[1]
    block_total = width_x * levels * width_y // gate_size
    total_cells = 3 * width_x * levels * width_y * devices
    total_gates = interp.shape[0] * devices * gate_size
    own_index = cell_block.reshape(devices, slots)
    own_alive = (
        jnp.arange(slots, dtype=jnp.int32)[None, :] < sweep_count.reshape(devices)[:, None]
    ).astype(jnp.int32)
    packed = jnp.stack([own_index, own_alive], 1)
    asked = lax.all_to_all(packed, RADAR_TILE, split_axis=0, concat_axis=0, tiled=True)
    asked_index = asked[:, 0, :].reshape(-1)
    local_alive = own_alive.reshape(-1).astype(jnp.float32)
    wind_field = background
    trace = []
    for step_index in range(ITERS):
        flat = wind_field.reshape(3, block_total, gate_size)
        empty = jnp.zeros((3, block_total, gate_size), jnp.float32)
        chosen = flat[:, asked_index, :].astype(jnp.bfloat16)
        arriving = joined_exchange(
            chosen.reshape(3, radar_count, tile_count, slots, gate_size),
            RADAR_TILE,
            (RADAR, TILE),
            (1, 2),
            (1, 2),
        )
        obs_cost, returned = observe(
            arriving.reshape(3, devices * slots, gate_size), interp, beam, observed, local_alive
        )
        landed = joined_exchange(
            returned.reshape(3, radar_count, tile_count, slots, gate_size),
            RADAR_TILE,
            (RADAR, TILE),
            (1, 2),
            (1, 2),
        )
        obs_cost, obs_flat = (
            obs_cost,
            empty.at[:, asked_index, :].add(landed.reshape(3, devices * slots, gate_size)),
        )
        obs_grad = obs_flat.reshape(wind_field.shape)
        spread, push = spread_faces(wind_field)
        offset = wind_field - background
        gradient = obs_grad + BACKGROUND_WEIGHT * offset + DIVERGENCE_WEIGHT * push
        local_cost = (
            obs_cost
            + 0.5 * BACKGROUND_WEIGHT * jnp.sum(offset * offset)
            + 0.5 * DIVERGENCE_WEIGHT * jnp.sum(spread * spread)
        )
        cost_sum, square_sum = (
            over_axes(local_cost, RADAR_TILE),
            over_axes(jnp.sum(gradient * gradient), RADAR_TILE),
        )
        scale = jnp.sqrt(square_sum / total_cells + EPSILON)
        wind_field = wind_field - STEP_LENGTH * gradient / scale
        trace.append(cost_sum / total_gates)
    faces = padded_2(wind_field, ((RADAR, 3), (TILE, 1)), 1)
    east_wind, north_wind, upward_wind = (faces[0], faces[1], faces[2])
    strain = jnp.stack(
        [
            along_x(east_wind),
            along_y(north_wind),
            along_z(upward_wind),
            0.5 * (along_y(east_wind) + along_x(north_wind)),
            0.5 * (along_z(east_wind) + along_x(upward_wind)),
            0.5 * (along_z(north_wind) + along_y(upward_wind)),
        ]
    )
    return (wind_field, strain, jnp.stack(trace))


def solution(mesh):
    torus = Mesh(mesh.devices.reshape(4, 2, 4, 4), ("radar_0", "radar_1", "tile_0", "tile_1"))
    in_specs = (
        P(None, TILE, None, RADAR),
        P(RADAR_TILE, None, None),
        P(RADAR_TILE, None, None),
        P(RADAR_TILE, None),
        P(RADAR_TILE),
        P(RADAR_TILE, None),
    )
    out_specs = (P(None, TILE, None, RADAR), P(None, TILE, None, RADAR), P())
    return jax.shard_map(
        shards, mesh=torus, in_specs=in_specs, out_specs=out_specs, check_vma=False
    )
```

profile of v0, /device:TPU:1, one launch (start us, length us, event | category | flops | bytes accessed | tf_op | source)
XLA Modules:
  0.0 330.2 jit_solution(9535569945727988790)
XLA Ops:
  15.4 11.6 %all-to-all-start = ((s32[128,2,2]{2,1,0:T(2,128)}), s32[128,2,2]{2,1,0:T(2,128)S(1)}, u32[]{:S(2)}, u32[]{:S(2)}) async-start(s32[128,2,2]{2,1,0:T(2,128)} %copy.39), calls=%async_computation | async-start | bytes 262144 | tf_op jit(solution)/shard_map/all_to_all | solution.py:119
  29.2 7.8 %all-to-all-done = s32[128,2,2]{2,1,0:T(2,128)S(1)} async-done(((s32[128,2,2]{2,1,0:T(2,128)}), s32[128,2,2]{2,1,0:T(2,128)S(1)}, u32[]{:S(2)}, u32[]{:S(2)}) %all-to-all-start) | async-done | bytes 2080 | tf_op jit(solution)/shard_map/all_to_all | solution.py:119
  55.4 7.9 %fusion = f32[256,128]{1,0:T(8,128)S(1)} fusion(bf16[3,256,128]{2,0,1:T(4,128)(2,1)S(1)} %bitcast.151, bf16[256,128,128]{2,1,0:T(8,128)(2,1)} %param.7, bf16[256,3,128]{2,0,1:T(8,128)(2,1)S(1)} %copy-done.4), kind=kOutput, calls=%fused_computation.24 | convolution fusion | flops 25427968 | bytes 8912896 | tf_op jit(solution)/shard_map/knc,ngc->nkg/dot_general | solution.py:85
  64.0 5.6 %fusion.66 = f32[256,3,128]{2,1,0:T(4,128)S(1)} fusion(bf16[256,128,128]{2,1,0:T(8,128)(2,1)} %param.7, f32[256,128]{1,0:T(8,128)S(1)} %get-tuple-element.20, bf16[256,3,128]{2,0,1:T(8,128)(2,1)S(1)} %copy-done.4), kind=kOutput, calls=%fused_computation.144 | convolution fusion | flops 25460736 | bytes 9109504 | tf_op jit(solution)/shard_map/nkg,ngc->knc/dot_general | solution.py:90
  70.6 10.3 %all-to-all-start.2 = ((f32[128,3,1,1,2,128]{5,4,3,2,1,0:T(2,128)}), f32[128,3,1,1,2,128]{5,4,3,2,1,0:T(2,128)S(1)}, u32[]{:S(2)}, u32[]{:S(2)}) async-start(f32[128,3,1,1,2,128]{5,4,3,2,1,0:T(2,128)} %bitcast.18), calls=%async_computation.2 | async-start | bytes 786432 | tf_op jit(solution)/shard_map/all_to_all | solution.py:56
  87.9 4.7 %collective-permute-done.5 = f32[16,32,1]{2,1,0:T(8,128)S(1)} collective-permute-done((f32[16,32,1]{2,1,0:T(8,128)S(1)}, f32[16,32,1]{2,1,0:T(8,128)S(1)}, u32[]{:S(2)}, u32[]{:S(2)}) %collective-permute-start.5) | collective-permute-done | bytes 2080 | tf_op jit(solution)/shard_map/ppermute | solution.py:28
  94.7 8.3 %scatter_fusion = f32[3,1024,128]{2,0,1:T(4,128)S(1)} fusion(f32[3,1024,128]{2,0,1:T(4,128)S(1)} %broadcast.90.clone, s32[256]{0:T(256)S(1)} %bitcast.159, f32[256,3,128]{2,1,0:T(4,128)S(1)} %bitcast.147), kind=kCustom, calls=%fused_computation.2 | custom fusion | flops 98304 | bytes 1180672 | tf_op jit(solution)/shard_map/scatter-add | solution.py:147
  109.1 7.8 %psum.112 = f32[]{:T(128)} all-reduce(f32[]{:T(128)} %multiply_reduce_fusion.3), channel_id=1, replica_groups=mesh['radar_0'=4,'radar_1'=2,'tile_0'=4,'tile_1'=4] {'radar_0'}, use_global_device_ids=true, to_apply=%region_3.4 | all-reduce | flops 1 | bytes 8 | tf_op jit(solution)/shard_map/psum | solution.py:63
  117.0 4.5 %psum.113 = f32[]{:T(128)} all-reduce(f32[]{:T(128)} %psum.112), channel_id=1, replica_groups=mesh['radar_0'=4,'radar_1'=2,'tile_0'=4,'tile_1'=4] {'radar_1'}, use_global_device_ids=true, to_apply=%region_4.5 | all-reduce | flops 1 | bytes 8 | tf_op jit(solution)/shard_map/psum | solution.py:63
  121.5 9.2 %psum.114 = f32[]{:T(128)} all-reduce(f32[]{:T(128)} %psum.113), channel_id=1, replica_groups=mesh['radar_0'=4,'radar_1'=2,'tile_0'=4,'tile_1'=4] {'tile_0'}, use_global_device_ids=true, to_apply=%region_5.6 | all-reduce | flops 1 | bytes 8 | tf_op jit(solution)/shard_map/psum | solution.py:63
  130.6 9.9 %psum.115 = f32[]{:T(128)} all-reduce(f32[]{:T(128)} %psum.114), channel_id=1, replica_groups=mesh['radar_0'=4,'radar_1'=2,'tile_0'=4,'tile_1'=4] {'tile_1'}, use_global_device_ids=true, to_apply=%region_6.7 | all-reduce | flops 1 | bytes 8 | tf_op jit(solution)/shard_map/psum | solution.py:63
  146.1 6.3 %collective-permute-start.10 = (f32[2,16,32,1]{3,2,1,0:T(8,128)}, f32[2,16,32,1]{3,2,1,0:T(8,128)}, u32[]{:S(2)}, u32[]{:S(2)}) collective-permute-start(f32[2,16,32,1]{3,2,1,0:T(8,128)} %get-tuple-element.40), channel_id=1, source_target_pairs={{16,0},{32,16},{48,32},{64,48},{80,64},{96,80},{112,96},{17,1},{33... | collective-permute-start | bytes 12296 | tf_op jit(solution)/shard_map/ppermute | solution.py:28
  155.6 4.6 %collective-permute-start.8 = (f32[2,1,32,256]{3,2,1,0:T(8,128)}, f32[2,1,32,256]{3,2,1,0:T(8,128)}, u32[]{:S(2)}, u32[]{:S(2)}) collective-permute-start(f32[2,1,32,256]{3,2,1,0:T(8,128)} %get-tuple-element.41), channel_id=1, source_target_pairs={{0,1},{1,2},{2,3},{3,4},{4,5},{5,6},{6,7},{7,8},{8,9},{9,10},{10,1... | collective-permute-start | bytes 196616 | tf_op jit(solution)/shard_map/ppermute | solution.py:27
  170.0 5.2 %all-to-all-start.3 = ((bf16[128,3,1,1,2,128]{5,4,3,2,1,0:T(2,128)(2,1)}), bf16[128,3,1,1,2,128]{5,4,3,2,1,0:T(2,128)(2,1)S(1)}, u32[]{:S(2)}, u32[]{:S(2)}) async-start(bf16[128,3,1,1,2,128]{5,4,3,2,1,0:T(2,128)(2,1)} %bitcast.157), calls=%async_computation.3 | async-start | bytes 393216 | tf_op jit(solution)/shard_map/all_to_all | solution.py:56
  182.3 4.8 %collective-permute-start.15 = (f32[1,32,256]{2,1,0:T(8,128)}, f32[1,32,256]{2,1,0:T(8,128)}, u32[]{:S(2)}, u32[]{:S(2)}) collective-permute-start(f32[1,32,256]{2,1,0:T(8,128)} %get-tuple-element.53), channel_id=1, source_target_pairs={{0,1},{1,2},{2,3},{3,4},{4,5},{5,6},{6,7},{7,8},{8,9},{9,10},{10,1... | collective-permute-start | bytes 98312 | tf_op jit(solution)/shard_map/ppermute | solution.py:27
  187.2 7.9 %fusion.1 = f32[256,128]{1,0:T(8,128)S(1)} fusion(bf16[3,256,128]{2,0,1:T(4,128)(2,1)S(1)} %bitcast.152, bf16[256,128,128]{2,1,0:T(8,128)(2,1)} %param.7, bf16[256,3,128]{2,0,1:T(8,128)(2,1)S(1)} %copy-done.4), kind=kOutput, calls=%fused_computation.25 | convolution fusion | flops 25427968 | bytes 8912896 | tf_op jit(solution)/shard_map/knc,ngc->nkg/dot_general | solution.py:85
  195.9 5.6 %fusion.64 = f32[256,3,128]{2,1,0:T(4,128)S(1)} fusion(bf16[256,128,128]{2,1,0:T(8,128)(2,1)} %param.7, f32[256,128]{1,0:T(8,128)S(1)} %get-tuple-element.25, bf16[256,3,128]{2,0,1:T(8,128)(2,1)S(1)} %copy-done.4), kind=kOutput, calls=%fused_computation.143 | convolution fusion | flops 25460736 | bytes 9109504 | tf_op jit(solution)/shard_map/nkg,ngc->knc/dot_general | solution.py:90
  202.5 12.0 %all-to-all-start.4 = ((f32[128,3,1,1,2,128]{5,4,3,2,1,0:T(2,128)}), f32[128,3,1,1,2,128]{5,4,3,2,1,0:T(2,128)S(1)}, u32[]{:S(2)}, u32[]{:S(2)}) async-start(f32[128,3,1,1,2,128]{5,4,3,2,1,0:T(2,128)} %bitcast.149), calls=%async_computation.4 | async-start | bytes 786432 | tf_op jit(solution)/shard_map/all_to_all | solution.py:56
  235.4 27.8 %scatter_fusion.1 = f32[3,1024,128]{2,0,1:T(4,128)} fusion(f32[3,1024,128]{2,0,1:T(4,128)} %broadcast.90, s32[256]{0:T(256)S(1)} %bitcast.160, f32[256,3,128]{2,1,0:T(4,128)} %bitcast.146), kind=kCustom, calls=%fused_computation.3 | custom fusion | flops 98304 | bytes 1180672 | tf_op jit(solution)/shard_map/scatter-add | solution.py:147
  272.9 7.9 %all-reduce.19 = (f32[]{:T(128)}, f32[]{:T(128)}, f32[]{:T(128)}) all-reduce(f32[]{:T(128)} %get-tuple-element.26, f32[]{:T(128)S(6)} %add.149, f32[]{:T(128)S(6)} %add.147), channel_id=1, replica_groups=mesh['radar_0'=4,'radar_1'=2,'tile_0'=4,'tile_1'=4] {'radar_0'}, use_global_device_ids=true, to_apply=%region_10.11 | all-reduce | flops 3 | bytes 24 | tf_op jit(solution)/shard_map/psum | solution.py:63
  280.7 4.7 %all-reduce.20 = (f32[]{:T(128)}, f32[]{:T(128)}, f32[]{:T(128)}) all-reduce(f32[]{:T(128)} %get-tuple-element.11, f32[]{:T(128)} %get-tuple-element.12, f32[]{:T(128)} %get-tuple-element.13), channel_id=1, replica_groups=mesh['radar_0'=4,'radar_1'=2,'tile_0'=4,'tile_1'=4] {'radar_1'}, use_global_device_ids=true, to_apply=%region_11.12 | all-reduce | flops 3 | bytes 24 | tf_op jit(solution)/shard_map/psum | solution.py:63
  285.5 9.2 %all-reduce.18 = (f32[]{:T(128)}, f32[]{:T(128)}, f32[]{:T(128)}) all-reduce(f32[]{:T(128)} %get-tuple-element.14, f32[]{:T(128)} %get-tuple-element.15, f32[]{:T(128)} %get-tuple-element.16), channel_id=1, replica_groups=mesh['radar_0'=4,'radar_1'=2,'tile_0'=4,'tile_1'=4] {'tile_0'}, use_global_device_ids=true, to_apply=%region_12.13 | all-reduce | flops 3 | bytes 24 | tf_op jit(solution)/shard_map/psum | solution.py:63
  294.6 9.8 %all-reduce.17 = (f32[]{:T(128)}, f32[]{:T(128)}, f32[]{:T(128)}) all-reduce(f32[]{:T(128)} %get-tuple-element.8, f32[]{:T(128)} %get-tuple-element.9, f32[]{:T(128)} %get-tuple-element.10), channel_id=1, replica_groups=mesh['radar_0'=4,'radar_1'=2,'tile_0'=4,'tile_1'=4] {'tile_1'}, use_global_device_ids=true, to_apply=%region_13.14 | all-reduce | flops 3 | bytes 24 | tf_op jit(solution)/shard_map/psum | solution.py:63
  309.4 5.5 %collective-permute-start.17 = (f32[3,16,32,1]{2,1,3,0:T(8,128)}, f32[3,16,32,1]{2,1,3,0:T(8,128)S(1)}, u32[]{:S(2)}, u32[]{:S(2)}) collective-permute-start(f32[3,16,32,1]{2,1,3,0:T(8,128)} %copy.53), channel_id=1, source_target_pairs={{0,16},{16,32},{32,48},{48,64},{64,80},{80,96},{96,112},{1,17},{17... | collective-permute-start | bytes 18440 | tf_op jit(solution)/shard_map/ppermute | solution.py:27
  (141 shorter events, 123.7 us)
Async XLA Ops:
  3.1 41.6 %collective-permute-start.1 = (f32[2,16,32,1]{3,2,1,0:T(8,128)}, f32[2,16,32,1]{3,2,1,0:T(8,128)}, u32[]{:S(2)}, u32[]{:S(2)}) collective-permute-start(f32[2,16,32,1]{3,2,1,0:T(8,128)} %get-tuple-element.43), channel_id=1, source_target_pairs={{0,16},{16,32},{32,48},{48,64},{64,80},{80,96},{96,112},{1,17},{17... | collective-permute-start | bytes 12296 | tf_op jit(solution)/shard_map/ppermute | solution.py:27
  7.6 37.1 %collective-permute-start.2 = (f32[2,16,32,1]{3,2,1,0:T(8,128)}, f32[2,16,32,1]{3,2,1,0:T(8,128)}, u32[]{:S(2)}, u32[]{:S(2)}) collective-permute-start(f32[2,16,32,1]{3,2,1,0:T(8,128)} %get-tuple-element.44), channel_id=1, source_target_pairs={{16,0},{32,16},{48,32},{64,48},{80,64},{96,80},{112,96},{17,1},{33... | collective-permute-start | bytes 12296 | tf_op jit(solution)/shard_map/ppermute | solution.py:28
  9.6 35.2 %collective-permute-start = (f32[2,1,32,256]{3,2,1,0:T(8,128)S(1)}, f32[2,1,32,256]{3,2,1,0:T(8,128)S(1)}, u32[]{:S(2)}, u32[]{:S(2)}) collective-permute-start(f32[2,1,32,256]{3,2,1,0:T(8,128)S(1)} %get-tuple-element.45), channel_id=1, source_target_pairs={{0,1},{1,2},{2,3},{3,4},{4,5},{5,6},{6,7},{7,8},{8,9},{9,10},{10,1... | collective-permute-start | bytes 196616 | tf_op jit(solution)/shard_map/ppermute | solution.py:27
  13.1 31.6 %collective-permute-start.3 = (f32[2,1,32,256]{3,2,1,0:T(8,128)S(1)}, f32[2,1,32,256]{3,2,1,0:T(8,128)S(1)}, u32[]{:S(2)}, u32[]{:S(2)}) collective-permute-start(f32[2,1,32,256]{3,2,1,0:T(8,128)S(1)} %get-tuple-element.46), channel_id=1, source_target_pairs={{1,0},{2,1},{3,2},{4,3},{5,4},{6,5},{7,6},{8,7},{9,8},{10,9},{11,1... | collective-permute-start | bytes 196616 | tf_op jit(solution)/shard_map/ppermute | solution.py:28
  15.4 21.6 %all-to-all-start = ((s32[128,2,2]{2,1,0:T(2,128)}), s32[128,2,2]{2,1,0:T(2,128)S(1)}, u32[]{:S(2)}, u32[]{:S(2)}) async-start(s32[128,2,2]{2,1,0:T(2,128)} %copy.39), calls=%async_computation | async-start | bytes 262144 | tf_op jit(solution)/shard_map/all_to_all | solution.py:119
  40.5 14.8 %all-to-all-start.1 = ((bf16[128,3,1,1,2,128]{5,4,3,2,1,0:T(2,128)(2,1)}), bf16[128,3,1,1,2,128]{5,4,3,2,1,0:T(2,128)(2,1)S(1)}, u32[]{:S(2)}, u32[]{:S(2)}) async-start(bf16[128,3,1,1,2,128]{5,4,3,2,1,0:T(2,128)(2,1)} %bitcast.7), calls=%async_computation.1 | async-start | bytes 393216 | tf_op jit(solution)/shard_map/all_to_all | solution.py:56
  47.8 44.7 %collective-permute-start.6 = (f32[1,32,256]{2,1,0:T(8,128)S(1)}, f32[1,32,256]{2,1,0:T(8,128)S(1)}, u32[]{:S(2)}, u32[]{:S(2)}) collective-permute-start(f32[1,32,256]{2,1,0:T(8,128)S(1)} %get-tuple-element.57), channel_id=1, source_target_pairs={{1,0},{2,1},{3,2},{4,3},{5,4},{6,5},{7,6},{8,7},{9,8},{10,9},{11,1... | collective-permute-start | bytes 98312 | tf_op jit(solution)/shard_map/ppermute | solution.py:28
  49.1 43.4 %collective-permute-start.7 = (f32[1,32,256]{2,1,0:T(8,128)S(1)}, f32[1,32,256]{2,1,0:T(8,128)S(1)}, u32[]{:S(2)}, u32[]{:S(2)}) collective-permute-start(f32[1,32,256]{2,1,0:T(8,128)S(1)} %get-tuple-element.58), channel_id=1, source_target_pairs={{0,1},{1,2},{2,3},{3,4},{4,5},{5,6},{6,7},{7,8},{8,9},{9,10},{10,1... | collective-permute-start | bytes 98312 | tf_op jit(solution)/shard_map/ppermute | solution.py:27
  70.6 23.6 %all-to-all-start.2 = ((f32[128,3,1,1,2,128]{5,4,3,2,1,0:T(2,128)}), f32[128,3,1,1,2,128]{5,4,3,2,1,0:T(2,128)S(1)}, u32[]{:S(2)}, u32[]{:S(2)}) async-start(f32[128,3,1,1,2,128]{5,4,3,2,1,0:T(2,128)} %bitcast.18), calls=%async_computation.2 | async-start | bytes 786432 | tf_op jit(solution)/shard_map/all_to_all | solution.py:56
  81.0 6.8 %collective-permute-start.4 = (f32[16,32,1]{2,1,0:T(8,128)S(1)}, f32[16,32,1]{2,1,0:T(8,128)S(1)}, u32[]{:S(2)}, u32[]{:S(2)}) collective-permute-start(f32[16,32,1]{2,1,0:T(8,128)S(1)} %get-tuple-element.60), channel_id=1, source_target_pairs={{0,16},{16,32},{32,48},{48,64},{64,80},{80,96},{96,112},{1,17},{17... | collective-permute-start | bytes 6152 | tf_op jit(solution)/shard_map/ppermute | solution.py:27
  84.6 8.0 %collective-permute-start.5 = (f32[16,32,1]{2,1,0:T(8,128)S(1)}, f32[16,32,1]{2,1,0:T(8,128)S(1)}, u32[]{:S(2)}, u32[]{:S(2)}) collective-permute-start(f32[16,32,1]{2,1,0:T(8,128)S(1)} %get-tuple-element.59), channel_id=1, source_target_pairs={{16,0},{32,16},{48,32},{64,48},{80,64},{96,80},{112,96},{17,1},{33... | collective-permute-start | bytes 6152 | tf_op jit(solution)/shard_map/ppermute | solution.py:28
  146.1 29.1 %collective-permute-start.10 = (f32[2,16,32,1]{3,2,1,0:T(8,128)}, f32[2,16,32,1]{3,2,1,0:T(8,128)}, u32[]{:S(2)}, u32[]{:S(2)}) collective-permute-start(f32[2,16,32,1]{3,2,1,0:T(8,128)} %get-tuple-element.40), channel_id=1, source_target_pairs={{16,0},{32,16},{48,32},{64,48},{80,64},{96,80},{112,96},{17,1},{33... | collective-permute-start | bytes 12296 | tf_op jit(solution)/shard_map/ppermute | solution.py:28
  152.4 22.9 %collective-permute-start.9 = (f32[2,16,32,1]{3,2,1,0:T(8,128)}, f32[2,16,32,1]{3,2,1,0:T(8,128)}, u32[]{:S(2)}, u32[]{:S(2)}) collective-permute-start(f32[2,16,32,1]{3,2,1,0:T(8,128)} %get-tuple-element.39), channel_id=1, source_target_pairs={{0,16},{16,32},{32,48},{48,64},{64,80},{80,96},{96,112},{1,17},{17... | collective-permute-start | bytes 12296 | tf_op jit(solution)/shard_map/ppermute | solution.py:27
  154.3 20.9 %collective-permute-start.11 = (f32[2,1,32,256]{3,2,1,0:T(8,128)}, f32[2,1,32,256]{3,2,1,0:T(8,128)}, u32[]{:S(2)}, u32[]{:S(2)}) collective-permute-start(f32[2,1,32,256]{3,2,1,0:T(8,128)} %get-tuple-element.42), channel_id=1, source_target_pairs={{1,0},{2,1},{3,2},{4,3},{5,4},{6,5},{7,6},{8,7},{9,8},{10,9},{11,1... | collective-permute-start | bytes 196616 | tf_op jit(solution)/shard_map/ppermute | solution.py:28
  155.6 19.7 %collective-permute-start.8 = (f32[2,1,32,256]{3,2,1,0:T(8,128)}, f32[2,1,32,256]{3,2,1,0:T(8,128)}, u32[]{:S(2)}, u32[]{:S(2)}) collective-permute-start(f32[2,1,32,256]{3,2,1,0:T(8,128)} %get-tuple-element.41), channel_id=1, source_target_pairs={{0,1},{1,2},{2,3},{3,4},{4,5},{5,6},{6,7},{7,8},{8,9},{9,10},{10,1... | collective-permute-start | bytes 196616 | tf_op jit(solution)/shard_map/ppermute | solution.py:27
  170.0 17.1 %all-to-all-start.3 = ((bf16[128,3,1,1,2,128]{5,4,3,2,1,0:T(2,128)(2,1)}), bf16[128,3,1,1,2,128]{5,4,3,2,1,0:T(2,128)(2,1)S(1)}, u32[]{:S(2)}, u32[]{:S(2)}) async-start(bf16[128,3,1,1,2,128]{5,4,3,2,1,0:T(2,128)(2,1)} %bitcast.157), calls=%async_computation.3 | async-start | bytes 393216 | tf_op jit(solution)/shard_map/all_to_all | solution.py:56
  181.0 46.9 %collective-permute-start.14 = (f32[1,32,256]{2,1,0:T(8,128)}, f32[1,32,256]{2,1,0:T(8,128)}, u32[]{:S(2)}, u32[]{:S(2)}) collective-permute-start(f32[1,32,256]{2,1,0:T(8,128)} %get-tuple-element.52), channel_id=1, source_target_pairs={{1,0},{2,1},{3,2},{4,3},{5,4},{6,5},{7,6},{8,7},{9,8},{10,9},{11,1... | collective-permute-start | bytes 98312 | tf_op jit(solution)/shard_map/ppermute | solution.py:28
  182.3 45.6 %collective-permute-start.15 = (f32[1,32,256]{2,1,0:T(8,128)}, f32[1,32,256]{2,1,0:T(8,128)}, u32[]{:S(2)}, u32[]{:S(2)}) collective-permute-start(f32[1,32,256]{2,1,0:T(8,128)} %get-tuple-element.53), channel_id=1, source_target_pairs={{0,1},{1,2},{2,3},{3,4},{4,5},{5,6},{6,7},{7,8},{8,9},{9,10},{10,1... | collective-permute-start | bytes 98312 | tf_op jit(solution)/shard_map/ppermute | solution.py:27
  202.5 30.4 %all-to-all-start.4 = ((f32[128,3,1,1,2,128]{5,4,3,2,1,0:T(2,128)}), f32[128,3,1,1,2,128]{5,4,3,2,1,0:T(2,128)S(1)}, u32[]{:S(2)}, u32[]{:S(2)}) async-start(f32[128,3,1,1,2,128]{5,4,3,2,1,0:T(2,128)} %bitcast.149), calls=%async_computation.4 | async-start | bytes 786432 | tf_op jit(solution)/shard_map/all_to_all | solution.py:56
  216.4 8.5 %collective-permute-start.12 = (f32[16,32,1]{2,1,0:T(8,128)}, f32[16,32,1]{2,1,0:T(8,128)}, u32[]{:S(2)}, u32[]{:S(2)}) collective-permute-start(f32[16,32,1]{2,1,0:T(8,128)} %get-tuple-element.55), channel_id=1, source_target_pairs={{0,16},{16,32},{32,48},{48,64},{64,80},{80,96},{96,112},{1,17},{17... | collective-permute-start | bytes 6152 | tf_op jit(solution)/shard_map/ppermute | solution.py:27
  219.9 8.0 %collective-permute-start.13 = (f32[16,32,1]{2,1,0:T(8,128)}, f32[16,32,1]{2,1,0:T(8,128)}, u32[]{:S(2)}, u32[]{:S(2)}) collective-permute-start(f32[16,32,1]{2,1,0:T(8,128)} %get-tuple-element.54), channel_id=1, source_target_pairs={{16,0},{32,16},{48,32},{64,48},{80,64},{96,80},{112,96},{17,1},{33... | collective-permute-start | bytes 6152 | tf_op jit(solution)/shard_map/ppermute | solution.py:28
  309.4 11.4 %collective-permute-start.17 = (f32[3,16,32,1]{2,1,3,0:T(8,128)}, f32[3,16,32,1]{2,1,3,0:T(8,128)S(1)}, u32[]{:S(2)}, u32[]{:S(2)}) collective-permute-start(f32[3,16,32,1]{2,1,3,0:T(8,128)} %copy.53), channel_id=1, source_target_pairs={{0,16},{16,32},{32,48},{48,64},{64,80},{80,96},{96,112},{1,17},{17... | collective-permute-start | bytes 18440 | tf_op jit(solution)/shard_map/ppermute | solution.py:27
  315.3 5.9 %collective-permute-start.18 = (f32[3,16,32,1]{2,1,3,0:T(8,128)S(1)}, f32[3,16,32,1]{2,1,3,0:T(8,128)}, u32[]{:S(2)}, u32[]{:S(2)}) collective-permute-start(f32[3,16,32,1]{2,1,3,0:T(8,128)S(1)} %copy.54), channel_id=1, source_target_pairs={{16,0},{32,16},{48,32},{64,48},{80,64},{96,80},{112,96},{17,1},{33... | collective-permute-start | bytes 18440 | tf_op jit(solution)/shard_map/ppermute | solution.py:28
  318.6 6.4 %collective-permute-start.19 = (f32[3,1,32,256]{3,2,1,0:T(8,128)S(1)}, f32[3,1,32,256]{3,2,1,0:T(8,128)S(1)}, u32[]{:S(2)}, u32[]{:S(2)}) collective-permute-start(f32[3,1,32,256]{3,2,1,0:T(8,128)S(1)} %get-tuple-element.38), channel_id=1, source_target_pairs={{1,0},{2,1},{3,2},{4,3},{5,4},{6,5},{7,6},{8,7},{9,8},{10,9},{11,1... | collective-permute-start | bytes 294920 | tf_op jit(solution)/shard_map/ppermute | solution.py:28
  (15 other events, 111.2 us)
where the time goes:
time: 333 us; the launch traced here: 330 us
  starting transfers between devices  102 us (31%)
  other arithmetic  65.3 us (20%)
  blocking collectives  62.9 us (19%)
  local copies, waits for them, and re-layouts  44.1 us (13%)
  matrix products  27 us (8%)
  waiting for transfers between devices  21.7 us (7%)
  between operations  7.59 us (2%)
    psum x8, blocking collectives, over_axes(): x = lax.psum(x, axis)  62.9 us
    ppermute x10, starting transfers between devices, padded_2(): lax.ppermute(last, axis, up)  37.3 us
    scatter-add x2, other arithmetic, shards(): empty.at[:, asked_index, :]  36.1 us
    all_to_all x4, starting transfers between devices, joined_exchange(): tiles = lax.all_to_all(tiles, axis, split_axis=0, concat_axis=0, tiled=True)  31.7 us
    ppermute x10, starting transfers between devices, padded_2(): lax.ppermute(first, axis, [(b, a) for a, b in up])  21 us
    dot_general x2, matrix products, observe(): jnp.einsum('knc,ngc->nkg', cell_rows, weights, preferred_element_type=jnp...  15.7 us
    all_to_all x1, starting transfers between devices, shards(): lax.all_to_all(packed, RADAR_TILE, split_axis=0, concat_axis=0, tiled=True)  11.6 us
    dot_general x2, matrix products, observe(): jnp.einsum('nkg,ngc->knc', adjoint, weights, preferred_element_type=jnp.f...  11.3 us
  transfers between devices with their start and end apart: 25, of which 6 were waited for; matrix products, arithmetic and copies ran while one was open for 19% of the time, Pallas kernels for 0%

commit v1 on v0

v1 whole, which is shorter than its diff:
```python
import functools

import jax
import jax.numpy as jnp
from jax import lax
from jax.experimental import pallas as pl
from jax.experimental.pallas import tpu as pltpu
from jax.sharding import PartitionSpec as P

BACKGROUND_WEIGHT = 0.5
DIVERGENCE_WEIGHT = 1.0
STEP_LENGTH = 0.3
EPSILON = 1e-06
GROUP = 8
LANES = 128
F32 = jnp.float32
BF16 = jnp.bfloat16
LOGICAL = pl.DeviceIdType.LOGICAL
BACK, SPREAD0, GRAD0, SPREAD1, GRAD1 = range(5)


def iota(shape, dim):
    return lax.broadcasted_iota(jnp.int32, shape, dim)


def kernel(sizes, bg_hbm, interp_hbm, codes_ref, beam_ref, looked_ref,
           wind_ref, strain_ref, cost_ref,
           weights, wind, grad0, grad1, spread0, spread1, push,
           codes_in, out1, in1, out2, in2, out3, in3, out4, in4, out5, in5,
           pick, place, field, misfit0, edges_out, edges_in,
           send_sems, recv_sems, halo_send, halo_recv, local_sems):
    n_radar, n_tile, total_cells, total_gates = sizes
    n = n_radar * n_tile
    nx, nz, ny = wind.shape[1] - 2, wind.shape[2], wind.shape[3]
    half = nx * nz
    r, t = lax.axis_index("radar"), lax.axis_index("tile")
    me = r * n_tile + t
    other = jnp.where(me + 1 >= n, me + 1 - n, me + 1)

    load_bg = pltpu.make_async_copy(bg_hbm, wind.at[:, pl.ds(1, nx)], local_sems.at[0])
    load_interp = pltpu.make_async_copy(interp_hbm, weights, local_sems.at[1])
    load_bg.start()
    load_interp.start()

    barrier = pltpu.get_barrier_semaphore()

    def greet(k, carry):
        d = me + k
        d = jnp.where(d >= n, d - n, d)
        pl.semaphore_signal(barrier, inc=1, device_id=d, device_id_type=LOGICAL)
        return carry

    lax.fori_loop(1, n, greet, 0)

    lane = iota((nz, LANES), 1)

    def pack_edges(stage, source, comps, one_field):
        def plane(x, carry):
            low, high = carry
            for k in range(comps):
                if one_field:
                    a, b = source[x + 1, :, :LANES], source[x + 1, :, ny - LANES :]
                else:
                    a, b = source[k, x + 1, :, :LANES], source[k, x + 1, :, ny - LANES :]
                to = 8 * x + k
                a = pltpu.roll(a, to, 1)
                b = pltpu.roll(b, to + 1, 1)
                low = jnp.where(lane == to, a, low)
                high = jnp.where(lane == to, b, high)
            return low, high

        zero = jnp.zeros((nz, LANES), F32)
        low, high = lax.fori_loop(0, nx, plane, (zero, zero))
        edges_out[stage, 0] = low
        edges_out[stage, 1] = high

    def halo_copies(stage, array, one_field):
        def planes(x):
            return array.at[x] if one_field else array.at[:, x]

        def make(i, src, dst, device):
            return pltpu.make_async_remote_copy(
                src_ref=src, dst_ref=dst,
                send_sem=halo_send.at[stage, i], recv_sem=halo_recv.at[stage, i],
                device_id=device, device_id_type=LOGICAL)

        up_t = jnp.where(t < n_tile - 1, me + 1, me - 1)
        down_t = jnp.where(t > 0, me - 1, me + 1)
        up_r = jnp.where(r < n_radar - 1, me + n_tile, me - n_tile)
        down_r = jnp.where(r > 0, me - n_tile, me + n_tile)
        return (
            (t < n_tile - 1, t > 0, make(0, planes(nx), planes(0), up_t)),
            (t > 0, t < n_tile - 1, make(1, planes(1), planes(nx + 1), down_t)),
            (r < n_radar - 1, r > 0, make(2, edges_out.at[stage, 1], edges_in.at[stage, 0], up_r)),
            (r > 0, r < n_radar - 1, make(3, edges_out.at[stage, 0], edges_in.at[stage, 1], down_r)),
        )

    def send_halos(stage, array, one_field=False):
        for i, (sends, receives, copy) in enumerate(halo_copies(stage, array, one_field)):
            pl.when(sends)(copy.start)

            @pl.when(jnp.logical_not(receives))
            def _():
                if i >= 2:
                    edges_in[stage, i - 2] = jnp.zeros((nz, LANES), F32)
                elif one_field:
                    array[(nx + 1) * i] = jnp.zeros((nz, ny), F32)
                else:
                    array[:, (nx + 1) * i] = jnp.zeros((3, nz, ny), F32)

    def await_halos(stage, array, one_field=False):
        for sends, receives, copy in halo_copies(stage, array, one_field):
            pl.when(sends)(copy.wait_send)
            pl.when(receives)(copy.wait_recv)

    def exchange_copy(stage, src, dst, d):
        return pltpu.make_async_remote_copy(
            src_ref=src.at[d], dst_ref=dst.at[me],
            send_sem=send_sems.at[stage], recv_sem=recv_sems.at[stage],
            device_id=d, device_id_type=LOGICAL)

    def send_all(stage, src, dst):
        def one(k, carry):
            d = me + k
            d = jnp.where(d >= n, d - n, d)
            exchange_copy(stage, src, dst, d).start()
            return carry

        lax.fori_loop(1, n, one, 0)
        dst[me] = src[me]

    def whole(stage, src, dst):
        return pltpu.make_async_remote_copy(
            src_ref=src.at[pl.ds(0, n - 1)], dst_ref=dst.at[pl.ds(0, n - 1)],
            send_sem=send_sems.at[stage], recv_sem=recv_sems.at[stage],
            device_id=other, device_id_type=LOGICAL)

    sub = iota((nz, ny), 0)
    wide = iota((nz, ny), 1)

    def diff_z(v):
        up = jnp.where(sub == nz - 1, 0.0, pltpu.roll(v, nz - 1, 0))
        down = jnp.where(sub == 0, 0.0, pltpu.roll(v, 1, 0))
        return 0.5 * (up - down)

    def diff_y(v, low, high, x, k):
        at = 8 * x + k
        low = pltpu.roll(low, lax.rem(LANES - at, LANES), 1)
        high = pltpu.roll(high, LANES - 1 - at, 1)
        up = jnp.where(wide == ny - 1, jnp.concatenate([high] * (ny // LANES), 1), pltpu.roll(v, ny - 1, 1))
        down = jnp.where(wide == 0, jnp.concatenate([low] * (ny // LANES), 1), pltpu.roll(v, 1, 1))
        return 0.5 * (up - down)

    def divergence(stage, source, out):
        low, high = edges_in[stage, 0], edges_in[stage, 1]

        def plane(x, total):
            s = (0.5 * (source[0, x + 2] - source[0, x]) + diff_y(source[1, x + 1], low, high, x, 1)
                 + diff_z(source[2, x + 1]))
            out[x + 1] = s
            return total + s * s

        return lax.fori_loop(0, nx, plane, jnp.zeros((nz, ny), F32))

    def pushes(stage, source, x, low, high):
        v = source[x + 1]
        return (0.5 * (source[x] - source[x + 2]), -diff_y(v, low, high, x, 0), -diff_z(v))

    def total_of(v):
        return jnp.sum(jnp.sum(v, axis=0, keepdims=True), axis=1, keepdims=True)

    def to_field(source):
        for h in range(ny // LANES):
            for k in range(3):
                v = source[k, 1 : nx + 1, :, h * LANES : (h + 1) * LANES]
                field[h * half : (h + 1) * half, k * LANES : (k + 1) * LANES] = v.reshape(half, LANES).astype(BF16)

    def gather(out, extra):
        chosen = jnp.dot(pick[...], field[...], preferred_element_type=F32)
        zero = jnp.zeros((n, LANES), F32)
        rows = []
        for k in range(2):
            for c in range(3):
                rows.append(chosen[k * n : (k + 1) * n, c * LANES : (c + 1) * LANES])
            rows.append(zero if k == 1 or extra is None else jnp.broadcast_to(extra, (n, LANES)))
        out[...] = jnp.swapaxes(jnp.stack(rows, 0), 0, 1).astype(BF16)

    def observe(source, out, dst, stage, step):
        def some(g, cost):
            for u in range(GROUP):
                d = g * GROUP + u
                both = weights[pl.ds(2 * d, 2)].reshape(2 * LANES, LANES)
                projected = lax.dot_general(source[d], both, (((1,), (1,)), ((), ())), preferred_element_type=F32)
                beams = beam_ref[d]
                radial = jnp.sum(beams * projected, axis=0, keepdims=True)
                if step is None:
                    misfit = radial - looked_ref[d]
                    misfit0[d] = misfit
                else:
                    misfit = misfit0[d] - step * radial
                cost = cost + misfit * misfit
                adjoint = (beams * misfit).astype(BF16)
                out[d] = jnp.dot(adjoint, both, preferred_element_type=F32).astype(BF16)
            return cost

        cost = lax.fori_loop(0, n // GROUP, some, jnp.zeros((1, 2 * LANES), F32))
        send_all(stage, out, dst)
        return 0.5 * jnp.sum(cost, axis=1, keepdims=True)

    def scatter(source, out):
        rows = jnp.swapaxes(source[...].astype(F32), 0, 1).astype(BF16)
        landed = jnp.concatenate(
            [jnp.concatenate([rows[4 * k + c] for c in range(3)], 1) for k in range(2)], 0)
        for h in range(ny // LANES):
            added = jnp.dot(place[h * half : (h + 1) * half], landed, preferred_element_type=F32)
            for c in range(3):
                lanes = slice(h * LANES, (h + 1) * LANES)
                v = added[:, c * LANES : (c + 1) * LANES].reshape(nx, nz, LANES)
                out[c, 1 : nx + 1, :, lanes] = v + push[c, :, :, lanes]

    def square_sum(source):
        def plane(x, total):
            for c in range(3):
                v = source[c, x + 1]
                total = total + v * v
            return total

        return total_of(lax.fori_loop(0, nx, plane, jnp.zeros((nz, ny), F32)))

    load_bg.wait()
    pack_edges(BACK, wind, 3, False)
    pl.semaphore_wait(barrier, n - 1)

    send_all(0, codes_ref, codes_in)
    send_halos(BACK, wind)
    to_field(wind)
    whole(0, codes_ref, codes_in).wait_recv()
    rows = jnp.swapaxes(codes_in[...].astype(F32), 0, 1)
    for k in range(2):
        code = (rows[4 * k] * LANES + rows[4 * k + 1]).astype(jnp.int32)
        across = jnp.transpose(code)
        for j in range(pick.shape[1] // LANES):
            hit = code == iota((n, LANES), 1) + j * LANES
            pick[k * n : (k + 1) * n, j * LANES : (j + 1) * LANES] = jnp.where(hit, 1.0, 0.0).astype(BF16)
            hit = across == iota((LANES, n), 0) + j * LANES
            place[j * LANES : (j + 1) * LANES, k * n : (k + 1) * n] = jnp.where(hit, 1.0, 0.0).astype(BF16)

    gather(out1, None)
    send_all(1, out1, in1)
    await_halos(BACK, wind)
    spread_cost0 = 0.5 * DIVERGENCE_WEIGHT * total_of(divergence(BACK, wind, spread0))
    pack_edges(SPREAD0, spread0, 1, True)
    send_halos(SPREAD0, spread0, True)
    load_interp.wait()
    whole(1, out1, in1).wait_recv()
    cost0 = observe(in1, out2, in2, 2, None) + spread_cost0
    await_halos(SPREAD0, spread0, True)
    low, high = edges_in[SPREAD0, 0], edges_in[SPREAD0, 1]

    def push_plane(x, carry):
        for c, v in enumerate(pushes(SPREAD0, spread0, x, low, high)):
            push[c, x] = DIVERGENCE_WEIGHT * v
        return carry

    lax.fori_loop(0, nx, push_plane, 0)
    whole(2, out2, in2).wait_recv()
    scatter(in2, grad0)
    squares = square_sum(grad0)
    to_field(grad0)

    first = squares.astype(BF16)
    rest = squares - first.astype(F32)
    second = rest.astype(BF16)
    third = (rest - second.astype(F32)).astype(BF16)
    at = iota((1, LANES), 1)
    extra = jnp.where(at == 0, first.astype(F32), jnp.where(at == 1, second.astype(F32), jnp.where(at == 2, third.astype(F32), 0.0)))
    gather(out3, extra)
    send_all(3, out3, in3)
    pack_edges(GRAD0, grad0, 3, False)
    send_halos(GRAD0, grad0)
    await_halos(GRAD0, grad0)
    divergence(GRAD0, grad0, spread1)
    pack_edges(SPREAD1, spread1, 1, True)
    send_halos(SPREAD1, spread1, True)
    whole(3, out3, in3).wait_recv()
    squares = jnp.sum(jnp.sum(in3[...].astype(F32), axis=0)[3:4], axis=1, keepdims=True)
    step0 = STEP_LENGTH / jnp.sqrt(squares / total_cells + EPSILON)
    cost1 = observe(in3, out4, in4, 4, step0)
    await_halos(SPREAD1, spread1, True)
    low1, high1 = edges_in[SPREAD1, 0], edges_in[SPREAD1, 1]

    def update_plane(x, carry):
        offsets, spreads = carry
        for c, v in enumerate(pushes(SPREAD1, spread1, x, low1, high1)):
            offset = -step0 * grad0[c, x + 1]
            offsets = offsets + offset * offset
            push[c, x] = push[c, x] - step0 * (DIVERGENCE_WEIGHT * v) + BACKGROUND_WEIGHT * offset
        spread = spread0[x + 1] - step0 * spread1[x + 1]
        return offsets, spreads + spread * spread

    zero = jnp.zeros((nz, ny), F32)
    offsets, spreads = lax.fori_loop(0, nx, update_plane, (zero, zero))
    cost1 = cost1 + 0.5 * total_of(BACKGROUND_WEIGHT * offsets + DIVERGENCE_WEIGHT * spreads)

    def wind_plane(x, carry):
        for c in range(3):
            wind[c, x] = wind[c, x] - step0 * grad0[c, x]
        return carry

    lax.fori_loop(0, nx + 2, wind_plane, 0)
    whole(4, out4, in4).wait_recv()
    scatter(in4, grad1)

    pack_edges(GRAD1, grad1, 3, False)
    send_halos(GRAD1, grad1)
    squares = square_sum(grad1)
    summary = jnp.where(at == 0, squares, jnp.where(at == 1, cost0, jnp.where(at == 2, cost1, 0.0)))

    def fill(d, carry):
        out5[d] = summary
        return carry

    lax.fori_loop(0, n, fill, 0)
    send_all(5, out5, in5)
    whole(5, out5, in5).wait_recv()
    sums = jnp.sum(in5[...], axis=0)
    cost_ref[...] = sums / total_gates
    squares = jnp.sum(jnp.where(at == 0, sums, 0.0), axis=1, keepdims=True)
    step1 = STEP_LENGTH / jnp.sqrt(squares / total_cells + EPSILON)
    await_halos(GRAD1, grad1)

    def last_plane(x, carry):
        for c in range(3):
            wind[c, x] = wind[c, x] - step1 * grad1[c, x]
        return carry

    lax.fori_loop(0, nx + 2, last_plane, 0)
    low, high = (edges_in[BACK, i] - step0 * edges_in[GRAD0, i] - step1 * edges_in[GRAD1, i] for i in range(2))

    def strain_plane(x, carry):
        v = [wind[c, x + 1] for c in range(3)]
        dx = [0.5 * (wind[c, x + 2] - wind[c, x]) for c in range(3)]
        dy = [diff_y(v[c], low, high, x, c) for c in range(3)]
        dz = [diff_z(v[c]) for c in range(3)]
        for c in range(3):
            wind_ref[c, x] = v[c]
        strain_ref[0, x] = dx[0]
        strain_ref[1, x] = dy[1]
        strain_ref[2, x] = dz[2]
        strain_ref[3, x] = 0.5 * (dy[0] + dx[1])
        strain_ref[4, x] = 0.5 * (dz[0] + dx[2])
        strain_ref[5, x] = 0.5 * (dz[1] + dy[2])
        return carry

    lax.fori_loop(0, nx, strain_plane, 0)

    pairs = ((codes_ref, codes_in), (out1, in1), (out2, in2), (out3, in3), (out4, in4), (out5, in5))
    for stage, (src, dst) in enumerate(pairs):
        whole(stage, src, dst).wait_send()


def shards(n_radar, n_tile, background, interp, beam, observed, cell_block, sweep_count):
    n = n_radar * n_tile
    _, nx, nz, ny = background.shape
    slots = interp.shape[0] // n
    gate = interp.shape[1]
    blocks = nx * nz * ny // gate
    total_cells = 3 * nx * nz * ny * n
    total_gates = interp.shape[0] * n * gate
    sizes = (n_radar, n_tile, total_cells, total_gates)
    across = ny // gate

    alive = jnp.arange(slots, dtype=jnp.int32)[None, :] < sweep_count.reshape(n)[:, None]
    index = cell_block.reshape(n, slots)
    code = (index % across) * (blocks // across) + index // across
    top = jnp.where(alive, code // LANES, -1)
    low = jnp.where(alive, code % LANES, 0)
    nothing = jnp.zeros_like(top)
    codes = jnp.stack([top, low, nothing, nothing], 2).reshape(n, 4 * slots)
    codes = jnp.broadcast_to(codes[:, :, None], (n, 4 * slots, LANES)).astype(BF16)
    live = alive.astype(F32)
    rays = beam.reshape(n, slots, 3, gate).astype(F32) * live[:, :, None, None]
    rays = jnp.pad(rays, ((0, 0), (0, 0), (0, 1), (0, 0)))
    own = jnp.arange(slots)[:, None] == jnp.arange(slots)[None, :]
    rays = jnp.where(own[None, :, None, :, None], rays[:, :, :, None, :], 0.0).reshape(n, 4 * slots, slots * gate)
    looked = (observed.reshape(n, slots, gate).astype(F32) * live[:, :, None]).reshape(n, 1, slots * gate)

    vmem = pl.BlockSpec(memory_space=pltpu.VMEM)
    hbm = pl.BlockSpec(memory_space=pl.ANY)
    message = pltpu.VMEM((n, 8, LANES), BF16)
    row = pltpu.VMEM((n, 1, LANES), F32)
    padded = pltpu.VMEM((3, nx + 2, nz, ny), F32)
    single = pltpu.VMEM((nx + 2, nz, ny), F32)
    wind, strain, cost = pl.pallas_call(
        functools.partial(kernel, sizes),
        name="wind_analysis",
        out_shape=(
            jax.ShapeDtypeStruct(background.shape, F32),
            jax.ShapeDtypeStruct((6, nx, nz, ny), F32),
            jax.ShapeDtypeStruct((1, LANES), F32),
        ),
        in_specs=[hbm, hbm, vmem, vmem, vmem],
        out_specs=(vmem, vmem, vmem),
        scratch_shapes=[
            pltpu.VMEM(interp.shape, BF16),
            padded, padded, padded, single, single,
            pltpu.VMEM((3, nx, nz, ny), F32),
            message, message, message, message, message, message, message, message, message, row, row,
            pltpu.VMEM((slots * n, blocks), BF16),
            pltpu.VMEM((blocks, slots * n), BF16),
            pltpu.VMEM((blocks, 3 * LANES), BF16),
            pltpu.VMEM((n, 1, slots * gate), F32),
            pltpu.VMEM((5, 2, nz, LANES), F32),
            pltpu.VMEM((5, 2, nz, LANES), F32),
            pltpu.SemaphoreType.DMA((6,)),
            pltpu.SemaphoreType.DMA((6,)),
            pltpu.SemaphoreType.DMA((5, 4)),
            pltpu.SemaphoreType.DMA((5, 4)),
            pltpu.SemaphoreType.DMA((2,)),
        ],
        compiler_params=pltpu.CompilerParams(
            collective_id=0, has_side_effects=True, vmem_limit_bytes=50 * 2**20),
    )(background, interp, codes, rays, looked)
    return wind, strain, cost[0, 1:3]


def solution(mesh):
    n_radar, n_tile = mesh.shape["radar"], mesh.shape["tile"]
    both = ("radar", "tile")
    in_specs = (
        P(None, "tile", None, "radar"), P(both, None, None), P(both, None, None),
        P(both, None), P(both), P(both, None))
    out_specs = (P(None, "tile", None, "radar"), P(None, "tile", None, "radar"), P())
    return jax.shard_map(
        functools.partial(shards, n_radar, n_tile), mesh=mesh, in_specs=in_specs, out_specs=out_specs, check_vma=False)
```

time: 333 us -> 127 us (0.38)
  Pallas kernels: 0 us -> 115 us
  starting transfers between devices: 102 us -> 0 us
  blocking collectives: 62.9 us -> 0 us
  other arithmetic: 65.3 us -> 3.84 us
  local copies, waits for them, and re-layouts: 44.1 us -> 7.33 us
  matrix products: 27 us -> 0 us
  waiting for transfers between devices: 21.7 us -> 0 us
  between operations: 7.59 us -> 0.74 us
    pallas_call x0 -> x1, Pallas kernels: none -> 115 us  [shards(): pl.pallas_call(functools.partial(kernel, sizes), name='wind_analysis', ou...]
    psum x8 -> x0, blocking collectives: 62.9 us -> none  [over_axes(): x = lax.psum(x, axis)]
    ppermute x20 -> x0, starting transfers between devices: 58.3 us -> none  [the longest x10 37.3 us: padded_2(): lax.ppermute(last, axis, up)]
    all_to_all x5 -> x0, starting transfers between devices: 43.3 us -> none  [the longest x4 31.7 us: joined_exchange(): tiles = lax.all_to_all(tiles, axis, split_axis=0, concat_axis=0, tiled=True)]
    scatter-add x2 -> x0, other arithmetic: 36.1 us -> none  [shards(): empty.at[:, asked_index, :]]
    dot_general x4 -> x0, matrix products: 27 us -> none  [the longest x2 15.7 us: observe(): jnp.einsum('knc,ngc->nkg', cell_rows, weights, preferred_element_type=jnp...]
    reduce_sum x7 -> x0, other arithmetic: 13.9 us -> none  [the longest x2 7.16 us: shards(): jnp.sum(gradient * gradient)]
    ppermute x20 -> x0, waiting for transfers between devices: 11.7 us -> none  [the longest x10 10.5 us: padded_2(): lax.ppermute(first, axis, [(b, a) for a, b in up])]
  transfers between devices with their start and end apart: 25 -> 0, of which waited for: 6 -> 0; matrix products, arithmetic and copies ran while one was open for 19% -> 0% of each run, Pallas kernels for 0% -> 0%
where the time goes in v1:
time: 127 us
  Pallas kernels  115 us (91%)
  local copies, waits for them, and re-layouts  7.33 us (6%)
  other arithmetic  3.84 us (3%)
    pallas_call x1, Pallas kernels, shards(): pl.pallas_call(functools.partial(kernel, sizes), name='wind_analysis', ou...  115 us
    unnamed x6, local copies, waits for them, and re-layouts  3.82 us

profile of v1, /device:TPU:1, one launch (start us, length us, event | category | flops | bytes accessed | tf_op | source)
XLA Modules:
  0.0 127.1 jit_solution(13820945988962322737)
XLA Ops:
  0.6 0.1 pad.7.clone
  0.7 0.1 broadcast_in_dim.42
  0.8 0.7 fusion.9
  1.6 0.8 reshape.351
  2.4 0.8 fusion.2
  3.2 0.1 copy.10
  3.2 0.1 copy.11
  3.3 0.1 maximum_maximum_fusion
  3.4 0.1 copy.12
  3.5 0.2 mul.46
  3.7 0.9 convert_element_type.42
  4.6 0.1 mul.48.looked_ref
  4.7 0.2 broadcast_in_dim.41.codes_ref
  5.0 1.1 convert_multiply_fusion
  6.1 0.3 copy.14
  6.4 0.1 pad.4.clone
  6.5 0.4 broadcast_in_dim.45
  6.9 0.8 broadcast_in_dim.46
  7.7 0.1 broadcast_select_fusion.beam_ref
  7.8 115.1 %wind_analysis.1 = (f32[3,16,32,256]{3,2,1,0:T(8,128)S(1)}, f32[6,16,32,256]{3,2,1,0:T(8,128)}, f32[1,128]{1,0:T(1,128)S(1)}) custom-call(f32[3,16,32,256]{3,2,1,0:T(8,128)} %bg_hbm.1, bf16[256,128,128]{2,1,0:T(8,128)(2,1)} %interp_hbm.1, bf16[128,8,128]{2,1,0:T(8,128)(2,1)S(1)} %broadcast_in_dim.41.codes_ref, ...), custom_call_target="tpu_custom_call" | custom-call | tf_op jit(solution)/shard_map/wind_analysis/pallas_call | solution.py:394
  122.9 0.6 slice_bitcast_fusion
  123.5 1.1 copy.20
  124.7 0.7 copy-done
  125.4 1.7 %copy.21 = f32[6,16,32,256]{3,2,1,0:T(8,128)} copy(f32[6,16,32,256]{3,2,1,0:T(8,128)S(1)} %copy-done) | data formatting | bytes 6291456
  (6 shorter events, 0.0 us)
Async XLA Ops:
  122.9 2.5 %copy-start = (f32[6,16,32,256]{3,2,1,0:T(8,128)S(1)}, f32[6,16,32,256]{3,2,1,0:T(8,128)}, u32[]{:S(2)}) copy-start(f32[6,16,32,256]{3,2,1,0:T(8,128)} %get-tuple-element.15) | copy-start | bytes 9437188

commit v2 on v1

v2 whole, which is shorter than its diff:
```python
import functools

import jax
import jax.numpy as jnp
from jax import lax
from jax.experimental import pallas as pl
from jax.experimental.pallas import tpu as pltpu
from jax.sharding import PartitionSpec as P

BACKGROUND_WEIGHT = 0.5
DIVERGENCE_WEIGHT = 1.0
STEP_LENGTH = 0.3
EPSILON = 1e-06
LANES = 128
F32 = jnp.float32
BF16 = jnp.bfloat16
LOGICAL = pl.DeviceIdType.LOGICAL
BACK, SPREAD0, GRAD0, SPREAD1, GRAD1 = range(5)


def iota(shape, dim):
    return lax.broadcasted_iota(jnp.int32, shape, dim)


def differences(nz, ny):
    sub = iota((nz, ny), 0)
    wide = iota((nz, ny), 1)

    def diff_z(v):
        up = jnp.where(sub == nz - 1, 0.0, pltpu.roll(v, nz - 1, 0))
        down = jnp.where(sub == 0, 0.0, pltpu.roll(v, 1, 0))
        return 0.5 * (up - down)

    def diff_y(v, low, high, x, k):
        at = 8 * x + k
        low = pltpu.roll(low, lax.rem(LANES - at, LANES), 1)
        high = pltpu.roll(high, LANES - 1 - at, 1)
        up = jnp.where(wide == ny - 1, jnp.concatenate([high] * (ny // LANES), 1), pltpu.roll(v, ny - 1, 1))
        down = jnp.where(wide == 0, jnp.concatenate([low] * (ny // LANES), 1), pltpu.roll(v, 1, 1))
        return 0.5 * (up - down)

    return diff_y, diff_z


def kernel(sizes, block_ref, count_ref, bg_hbm, interp_hbm, beam_hbm, looked_hbm,
           wind_ref, edges_ref, cost_ref,
           weights, beams16, looked16, wind, grad0, grad1, spread0, spread1, push,
           codes_out, codes_in, out1, in1, out2, in2, out3, in3, out4, in4, out5, in5,
           pick, place, field, beams32, looked32, rays, looked, misfit0, edges_out, edges_in,
           send_sems, recv_sems, halo_send, halo_recv, local_sems):
    n_radar, n_tile, total_cells, total_gates = sizes
    n = n_radar * n_tile
    nx, nz, ny = wind.shape[1] - 2, wind.shape[2], wind.shape[3]
    half = nx * nz
    group = min(16, n // 2)
    r, t = lax.axis_index("radar"), lax.axis_index("tile")
    me = r * n_tile + t
    other = jnp.where(me + 1 >= n, me + 1 - n, me + 1)

    load_bg = pltpu.make_async_copy(bg_hbm, wind.at[:, pl.ds(1, nx)], local_sems.at[0])
    load_interp = pltpu.make_async_copy(interp_hbm, weights, local_sems.at[1])
    load_beams = pltpu.make_async_copy(beam_hbm, beams16, local_sems.at[2])
    load_looked = pltpu.make_async_copy(looked_hbm, looked16, local_sems.at[3])
    load_bg.start()
    load_beams.start()
    load_looked.start()
    load_interp.start()

    barrier = pltpu.get_barrier_semaphore()

    def greet(k, carry):
        d = me + k
        d = jnp.where(d >= n, d - n, d)
        pl.semaphore_signal(barrier, inc=1, device_id=d, device_id_type=LOGICAL)
        return carry

    lax.fori_loop(1, n, greet, 0)

    def around(k):
        d = me + k
        return jnp.where(d >= n, d - n, d)

    def back_from(k):
        d = me - k
        return jnp.where(d < 0, d + n, d)

    lane = iota((nz, LANES), 1)

    def pack_edges(stage, source, comps, one_field):
        def plane(x, carry):
            low, high = carry
            for k in range(comps):
                if one_field:
                    a, b = source[x + 1, :, :LANES], source[x + 1, :, ny - LANES :]
                else:
                    a, b = source[k, x + 1, :, :LANES], source[k, x + 1, :, ny - LANES :]
                to = 8 * x + k
                a = pltpu.roll(a, to, 1)
                b = pltpu.roll(b, to + 1, 1)
                low = jnp.where(lane == to, a, low)
                high = jnp.where(lane == to, b, high)
            return low, high

        zero = jnp.zeros((nz, LANES), F32)
        low, high = lax.fori_loop(0, nx, plane, (zero, zero))
        edges_out[stage, 0] = low
        edges_out[stage, 1] = high

    def halo_copies(stage, array, one_field):
        def planes(x):
            return array.at[x] if one_field else array.at[:, x]

        def make(i, src, dst, device):
            return pltpu.make_async_remote_copy(
                src_ref=src, dst_ref=dst,
                send_sem=halo_send.at[stage, i], recv_sem=halo_recv.at[stage, i],
                device_id=device, device_id_type=LOGICAL)

        up_t = jnp.where(t < n_tile - 1, me + 1, me - 1)
        down_t = jnp.where(t > 0, me - 1, me + 1)
        up_r = jnp.where(r < n_radar - 1, me + n_tile, me - n_tile)
        down_r = jnp.where(r > 0, me - n_tile, me + n_tile)
        return (
            (t < n_tile - 1, t > 0, make(0, planes(nx), planes(0), up_t)),
            (t > 0, t < n_tile - 1, make(1, planes(1), planes(nx + 1), down_t)),
            (r < n_radar - 1, r > 0, make(2, edges_out.at[stage, 1], edges_in.at[stage, 0], up_r)),
            (r > 0, r < n_radar - 1, make(3, edges_out.at[stage, 0], edges_in.at[stage, 1], down_r)),
        )

    def send_halos(stage, array, one_field=False):
        for i, (sends, receives, copy) in enumerate(halo_copies(stage, array, one_field)):
            pl.when(sends)(copy.start)

            @pl.when(jnp.logical_not(receives))
            def _():
                if i >= 2:
                    edges_in[stage, i - 2] = jnp.zeros((nz, LANES), F32)
                elif one_field:
                    array[(nx + 1) * i] = jnp.zeros((nz, ny), F32)
                else:
                    array[:, (nx + 1) * i] = jnp.zeros((3, nz, ny), F32)

    def await_halos(stage, array, one_field=False):
        for sends, receives, copy in halo_copies(stage, array, one_field):
            pl.when(sends)(copy.wait_send)
            pl.when(receives)(copy.wait_recv)

    def exchange_copy(stage, src, dst, d, part):
        return pltpu.make_async_remote_copy(
            src_ref=src.at[d], dst_ref=dst.at[me],
            send_sem=send_sems.at[stage], recv_sem=recv_sems.at[stage, part],
            device_id=d, device_id_type=LOGICAL)

    def send_all(stage, src, dst, parts):
        def one(k, carry):
            exchange_copy(stage, src, dst, around(k), k // group if parts else 0).start()
            return carry

        lax.fori_loop(1, n, one, 0)
        dst[me] = src[me]

    def whole(stage, src, dst, part=0, count=n - 1):
        return pltpu.make_async_remote_copy(
            src_ref=src.at[pl.ds(0, count)], dst_ref=dst.at[pl.ds(0, count)],
            send_sem=send_sems.at[stage], recv_sem=recv_sems.at[stage, part],
            device_id=other, device_id_type=LOGICAL)

    diff_y, diff_z = differences(nz, ny)

    def divergence(stage, source, out):
        low, high = edges_in[stage, 0], edges_in[stage, 1]

        def plane(x, total):
            s = (0.5 * (source[0, x + 2] - source[0, x]) + diff_y(source[1, x + 1], low, high, x, 1)
                 + diff_z(source[2, x + 1]))
            out[x + 1] = s
            return total + s * s

        return lax.fori_loop(0, nx, plane, jnp.zeros((nz, ny), F32))

    def pushes(stage, source, x, low, high):
        v = source[x + 1]
        return (0.5 * (source[x] - source[x + 2]), -diff_y(v, low, high, x, 0), -diff_z(v))

    def total_of(v):
        return jnp.sum(jnp.sum(v, axis=0, keepdims=True), axis=1, keepdims=True)

    def to_field(source):
        for h in range(ny // LANES):
            for k in range(3):
                v = source[k, 1 : nx + 1, :, h * LANES : (h + 1) * LANES]
                field[h * half : (h + 1) * half, k * LANES : (k + 1) * LANES] = v.reshape(half, LANES).astype(BF16)

    def gather(out, extra):
        chosen = jnp.dot(pick[...], field[...], preferred_element_type=F32)
        zero = jnp.zeros((n, LANES), F32)
        rows = []
        for k in range(2):
            for c in range(3):
                rows.append(chosen[k * n : (k + 1) * n, c * LANES : (c + 1) * LANES])
            rows.append(zero if k == 1 or extra is None else jnp.broadcast_to(extra, (n, LANES)))
        out[...] = jnp.swapaxes(jnp.stack(rows, 0), 0, 1).astype(BF16)

    def observe(source, out, dst, stage, step):
        def some(q, cost, first):
            ds = [back_from(q * group + u) for u in range(group)]
            both = [weights[pl.ds(2 * d, 2)].reshape(2 * LANES, LANES) for d in ds]
            projected = [
                lax.dot_general(source[d], w, (((1,), (1,)), ((), ())), preferred_element_type=F32)
                for d, w in zip(ds, both)]
            beams = [rays[d] for d in ds]
            radial = [jnp.sum(b * p, axis=0, keepdims=True) for b, p in zip(beams, projected)]
            if step is None:
                misfit = [x - looked[d] for d, x in zip(ds, radial)]
                for d, x in zip(ds, misfit):
                    misfit0[d] = x
            else:
                misfit = [misfit0[d] - step * x for d, x in zip(ds, radial)]
            for x in misfit:
                cost = cost + x * x
            adjoint = [(b * x).astype(BF16) for b, x in zip(beams, misfit)]
            back = [jnp.dot(x, w, preferred_element_type=F32) for x, w in zip(adjoint, both)]
            for d, x in zip(ds, back):
                out[d] = x.astype(BF16)
            for u, d in enumerate(ds):
                if first and u == 0:
                    dst[d] = out[d]
                else:
                    exchange_copy(stage, out, dst, d, 0).start()
            return cost

        def later(q, cost):
            if step is None:
                whole(stage - 1, out, source, q, group).wait_recv()
            return some(q, cost, False)

        cost = jnp.zeros((1, 2 * LANES), F32)
        if step is None:
            whole(stage - 1, out, source, 0, group - 1).wait_recv()
        cost = some(0, cost, True)
        cost = lax.fori_loop(1, n // group, later, cost)
        return 0.5 * jnp.sum(cost, axis=1, keepdims=True)

    def scatter(source, out, to_field):
        rows = jnp.swapaxes(source[...].astype(F32), 0, 1).astype(BF16)
        landed = jnp.concatenate(
            [jnp.concatenate([rows[4 * k + c] for c in range(3)], 1) for k in range(2)], 0)
        total = jnp.zeros((nz, LANES), F32)
        for h in range(ny // LANES):
            added = jnp.dot(place[h * half : (h + 1) * half], landed, preferred_element_type=F32)
            for c in range(3):
                lanes = slice(h * LANES, (h + 1) * LANES)
                v = added[:, c * LANES : (c + 1) * LANES].reshape(nx, nz, LANES) + push[c, :, :, lanes]
                out[c, 1 : nx + 1, :, lanes] = v
                total = total + jnp.sum(v * v, axis=0)
                if to_field:
                    field[h * half : (h + 1) * half, c * LANES : (c + 1) * LANES] = v.reshape(half, LANES).astype(BF16)
        return total_of(total)

    def code_row(d, carry):
        count = count_ref[0, d]

        def code(k):
            b = block_ref[2 * d + k]
            c = lax.rem(b, ny // LANES) * half + lax.div(b, ny // LANES)
            return jnp.where(k < count, c, -1)

        codes_out[d] = jnp.where(iota((1, LANES), 1) < LANES // 2, code(0), code(1))
        return carry

    lax.fori_loop(0, n, code_row, 0)
    load_bg.wait()
    pack_edges(BACK, wind, 3, False)
    pl.semaphore_wait(barrier, n - 1)
    send_all(0, codes_out, codes_in, False)
    send_halos(BACK, wind)
    to_field(wind)

    load_beams.wait()
    load_looked.wait()
    beams32[...] = beams16[...].astype(F32)
    looked32[...] = looked16[...].astype(F32)
    zero = jnp.zeros((n, LANES), F32)
    rows = []
    for k in range(2):
        rows += [beams32[c, pl.ds(k, n, stride=2), :] for c in range(3)] + [zero]
    out_row = jnp.swapaxes(jnp.stack(rows, 0), 0, 1)
    rays[:, :, :LANES] = out_row
    eight = iota((8, LANES), 0)

    def ray_rows(q, carry):
        ds = [q * 8 + u for u in range(8)]
        counts = [count_ref[0, d] for d in ds]
        values = [rays[d, :, :LANES] for d in ds]
        seen = [[looked32[pl.ds(2 * d + k, 1), :] for k in range(2)] for d in ds]
        for d, count, v, s in zip(ds, counts, values, seen):
            rays[d, :, :LANES] = jnp.where((eight < 4) & (count > 0), v, 0.0)
            rays[d, :, LANES:] = jnp.where((eight >= 4) & (count > 1), v, 0.0)
            looked[d] = jnp.concatenate([jnp.where(count > k, s[k], 0.0) for k in range(2)], 1)
        return carry

    lax.fori_loop(0, n // 8, ray_rows, 0)

    whole(0, codes_out, codes_in).wait_recv()
    codes = codes_in[...].reshape(n, LANES)
    turned = pltpu.roll(codes, LANES // 2, 1)
    front = iota((n, LANES), 1) < LANES // 2
    code = (jnp.where(front, codes, turned), jnp.where(front, turned, codes))
    for k in range(2):
        for j in range(pick.shape[1] // LANES):
            hit = code[k] == iota((n, LANES), 1) + j * LANES
            pick[k * n : (k + 1) * n, j * LANES : (j + 1) * LANES] = jnp.where(hit, 1.0, 0.0).astype(BF16)

    gather(out1, None)
    send_all(1, out1, in1, True)
    for k in range(2):
        across = jnp.transpose(code[k])
        for j in range(pick.shape[1] // LANES):
            hit = across == iota((LANES, n), 0) + j * LANES
            place[j * LANES : (j + 1) * LANES, k * n : (k + 1) * n] = jnp.where(hit, 1.0, 0.0).astype(BF16)
    await_halos(BACK, wind)
    spread_cost0 = 0.5 * DIVERGENCE_WEIGHT * total_of(divergence(BACK, wind, spread0))
    pack_edges(SPREAD0, spread0, 1, True)
    send_halos(SPREAD0, spread0, True)
    load_interp.wait()
    cost0 = observe(in1, out2, in2, 2, None) + spread_cost0
    await_halos(SPREAD0, spread0, True)
    low, high = edges_in[SPREAD0, 0], edges_in[SPREAD0, 1]

    def push_plane(x, carry):
        for c, v in enumerate(pushes(SPREAD0, spread0, x, low, high)):
            push[c, x] = DIVERGENCE_WEIGHT * v
        return carry

    lax.fori_loop(0, nx, push_plane, 0)
    whole(2, out2, in2).wait_recv()
    squares = scatter(in2, grad0, True)

    first = squares.astype(BF16)
    rest = squares - first.astype(F32)
    second = rest.astype(BF16)
    third = (rest - second.astype(F32)).astype(BF16)
    at = iota((1, LANES), 1)
    extra = jnp.where(at == 0, first.astype(F32), jnp.where(at == 1, second.astype(F32), jnp.where(at == 2, third.astype(F32), 0.0)))
    gather(out3, extra)
    send_all(3, out3, in3, False)
    pack_edges(GRAD0, grad0, 3, False)
    send_halos(GRAD0, grad0)
    whole(3, out3, in3).wait_recv()
    squares = jnp.sum(jnp.sum(in3[...].astype(F32), axis=0)[3:4], axis=1, keepdims=True)
    step0 = STEP_LENGTH / jnp.sqrt(squares / total_cells + EPSILON)
    cost1 = observe(in3, out4, in4, 4, step0)
    await_halos(GRAD0, grad0)
    divergence(GRAD0, grad0, spread1)
    pack_edges(SPREAD1, spread1, 1, True)
    send_halos(SPREAD1, spread1, True)

    def wind_plane(x, carry):
        for c in range(3):
            wind[c, x] = wind[c, x] - step0 * grad0[c, x]
        return carry

    lax.fori_loop(0, nx + 2, wind_plane, 0)
    await_halos(SPREAD1, spread1, True)
    low1, high1 = edges_in[SPREAD1, 0], edges_in[SPREAD1, 1]

    def update_plane(x, carry):
        offsets, spreads = carry
        for c, v in enumerate(pushes(SPREAD1, spread1, x, low1, high1)):
            offset = -step0 * grad0[c, x + 1]
            offsets = offsets + offset * offset
            push[c, x] = push[c, x] - step0 * (DIVERGENCE_WEIGHT * v) + BACKGROUND_WEIGHT * offset
        spread = spread0[x + 1] - step0 * spread1[x + 1]
        return offsets, spreads + spread * spread

    zero = jnp.zeros((nz, ny), F32)
    offsets, spreads = lax.fori_loop(0, nx, update_plane, (zero, zero))
    cost1 = cost1 + 0.5 * total_of(BACKGROUND_WEIGHT * offsets + DIVERGENCE_WEIGHT * spreads)
    whole(4, out4, in4).wait_recv()
    squares = scatter(in4, grad1, False)

    summary = jnp.where(at == 0, squares, jnp.where(at == 1, cost0, jnp.where(at == 2, cost1, 0.0)))

    def fill(d, carry):
        out5[d] = summary
        return carry

    lax.fori_loop(0, n, fill, 0)
    send_all(5, out5, in5, False)
    pack_edges(GRAD1, grad1, 3, False)
    send_halos(GRAD1, grad1)
    whole(5, out5, in5).wait_recv()
    sums = jnp.sum(in5[...], axis=0)
    cost_ref[...] = sums / total_gates
    squares = jnp.sum(jnp.where(at == 0, sums, 0.0), axis=1, keepdims=True)
    step1 = STEP_LENGTH / jnp.sqrt(squares / total_cells + EPSILON)
    await_halos(GRAD1, grad1)

    def last_plane(x, carry):
        for c in range(3):
            wind_ref[c, x] = wind[c, x] - step1 * grad1[c, x]
        return carry

    lax.fori_loop(0, nx + 2, last_plane, 0)
    for i in range(2):
        edges_ref[i] = edges_in[BACK, i] - step0 * edges_in[GRAD0, i] - step1 * edges_in[GRAD1, i]

    pairs = ((codes_out, codes_in), (out1, in1), (out2, in2), (out3, in3), (out4, in4), (out5, in5))
    for stage, (src, dst) in enumerate(pairs):
        whole(stage, src, dst).wait_send()


def strain_kernel(planes, cost_ref, wind_ref, edges_ref, final_ref, strain_ref, trace_ref):
    nz, ny = wind_ref.shape[2:]
    start = pl.program_id(0) * planes
    diff_y, diff_z = differences(nz, ny)
    low, high = edges_ref[0], edges_ref[1]
    trace_ref[0] = cost_ref[0, 1]
    trace_ref[1] = cost_ref[0, 2]

    def plane(i, carry):
        x = start + i
        v = [wind_ref[c, x + 1] for c in range(3)]
        dx = [0.5 * (wind_ref[c, x + 2] - wind_ref[c, x]) for c in range(3)]
        dy = [diff_y(v[c], low, high, x, c) for c in range(3)]
        dz = [diff_z(v[c]) for c in range(3)]
        for c in range(3):
            final_ref[c, i] = v[c]
        strain_ref[0, i] = dx[0]
        strain_ref[1, i] = dy[1]
        strain_ref[2, i] = dz[2]
        strain_ref[3, i] = 0.5 * (dy[0] + dx[1])
        strain_ref[4, i] = 0.5 * (dz[0] + dx[2])
        strain_ref[5, i] = 0.5 * (dz[1] + dy[2])
        return carry

    lax.fori_loop(0, planes, plane, 0)


def shards(n_radar, n_tile, background, interp, beam, observed, cell_block, sweep_count):
    n = n_radar * n_tile
    _, nx, nz, ny = background.shape
    slots = interp.shape[0] // n
    gate = interp.shape[1]
    blocks = nx * nz * ny // gate
    total_cells = 3 * nx * nz * ny * n
    total_gates = interp.shape[0] * n * gate
    sizes = (n_radar, n_tile, total_cells, total_gates)

    vmem = pl.BlockSpec(memory_space=pltpu.VMEM)
    smem = pl.BlockSpec(memory_space=pltpu.SMEM)
    hbm = pl.BlockSpec(memory_space=pl.ANY)
    message = pltpu.VMEM((n, 8, LANES), BF16)
    row = pltpu.VMEM((n, 1, LANES), F32)
    code_row = pltpu.VMEM((n, 1, LANES), jnp.int32)
    padded = pltpu.VMEM((3, nx + 2, nz, ny), F32)
    single = pltpu.VMEM((nx + 2, nz, ny), F32)
    rays = jnp.transpose(beam, (1, 0, 2))
    groups = n // min(16, n // 2)
    wind, edges, cost = pl.pallas_call(
        functools.partial(kernel, sizes),
        name="wind_analysis",
        out_shape=(
            jax.ShapeDtypeStruct((3, nx + 2, nz, ny), F32),
            jax.ShapeDtypeStruct((2, nz, LANES), F32),
            jax.ShapeDtypeStruct((1, LANES), F32),
        ),
        in_specs=[smem, smem, hbm, hbm, hbm, hbm],
        out_specs=(vmem, vmem, vmem),
        scratch_shapes=[
            pltpu.VMEM(interp.shape, BF16),
            pltpu.VMEM(rays.shape, BF16),
            pltpu.VMEM(observed.shape, BF16),
            padded, padded, padded, single, single,
            pltpu.VMEM((3, nx, nz, ny), F32),
            code_row, code_row, message, message, message, message, message, message, message, message, row, row,
            pltpu.VMEM((slots * n, blocks), BF16),
            pltpu.VMEM((blocks, slots * n), BF16),
            pltpu.VMEM((blocks, 3 * LANES), BF16),
            pltpu.VMEM(rays.shape, F32),
            pltpu.VMEM(observed.shape, F32),
            pltpu.VMEM((n, 8, slots * gate), F32),
            pltpu.VMEM((n, 1, slots * gate), F32),
            pltpu.VMEM((n, 1, slots * gate), F32),
            pltpu.VMEM((5, 2, nz, LANES), F32),
            pltpu.VMEM((5, 2, nz, LANES), F32),
            pltpu.SemaphoreType.DMA((6,)),
            pltpu.SemaphoreType.DMA((6, groups)),
            pltpu.SemaphoreType.DMA((5, 4)),
            pltpu.SemaphoreType.DMA((5, 4)),
            pltpu.SemaphoreType.DMA((4,)),
        ],
        compiler_params=pltpu.CompilerParams(
            collective_id=0, has_side_effects=True, vmem_limit_bytes=50 * 2**20),
    )(cell_block, sweep_count, background, interp, rays, observed)

    planes = nx // 4
    return pl.pallas_call(
        functools.partial(strain_kernel, planes),
        name="strain",
        grid=(nx // planes,),
        out_shape=(
            jax.ShapeDtypeStruct(background.shape, F32),
            jax.ShapeDtypeStruct((6, nx, nz, ny), F32),
            jax.ShapeDtypeStruct((2,), F32),
        ),
        in_specs=[smem, vmem, vmem],
        out_specs=(
            pl.BlockSpec((3, planes, nz, ny), lambda i: (0, i, 0, 0)),
            pl.BlockSpec((6, planes, nz, ny), lambda i: (0, i, 0, 0)),
            smem,
        ),
        compiler_params=pltpu.CompilerParams(vmem_limit_bytes=24 * 2**20),
    )(cost, wind, edges)


def solution(mesh):
    n_radar, n_tile = mesh.shape["radar"], mesh.shape["tile"]
    both = ("radar", "tile")
    in_specs = (
        P(None, "tile", None, "radar"), P(both, None, None), P(both, None, None),
        P(both, None), P(both), P(both, None))
    out_specs = (P(None, "tile", None, "radar"), P(None, "tile", None, "radar"), P())
    return jax.shard_map(
        functools.partial(shards, n_radar, n_tile), mesh=mesh, in_specs=in_specs, out_specs=out_specs, check_vma=False)
```

time: 127 us -> 75.5 us (0.59)
  Pallas kernels: 115 us -> 70.1 us
  other arithmetic: 3.84 us -> 0 us
  local copies, waits for them, and re-layouts: 7.33 us -> 4.5 us
    pallas_call x1, Pallas kernels: 115 us -> 65.7 us  [shards(): pl.pallas_call(functools.partial(kernel, sizes), name='wind_analysis', ou...]
    pallas_call x0 -> x1, Pallas kernels: none -> 4.44 us  [shards(): pl.pallas_call(functools.partial(strain_kernel, planes), name='strain', g...]
    convert_element_type x2 -> x0, other arithmetic: 1.59 us -> none  [the longest x1 0.86 us: shards(): observed.reshape(n, slots, gate).astype(F32) * live[:, :, None]]
    broadcast_in_dim x4 -> x0, local copies, waits for them, and re-layouts: 1.48 us -> none  [the longest x3 1.28 us: shards(): jnp.where(own[None, :, None, :, None], rays[:, :, :, None, :], 0.0)]
    mul x2 -> x0, other arithmetic: 1.28 us -> none  [the longest x1 1.14 us: shards(): rays = beam.reshape(n, slots, 3, gate).astype(F32) * live[:, :, None, None]]
    unnamed x6 -> x10, local copies, waits for them, and re-layouts: 3.82 us -> 4.5 us
where the time goes in v2:
time: 75.5 us; the launch traced here: 75.3 us
  Pallas kernels  70.1 us (93%)
  local copies, waits for them, and re-layouts  4.5 us (6%)
    pallas_call x1, Pallas kernels, shards(): pl.pallas_call(functools.partial(kernel, sizes), name='wind_analysis', ou...  65.7 us
    unnamed x10, local copies, waits for them, and re-layouts  4.5 us
    pallas_call x1, Pallas kernels, shards(): pl.pallas_call(functools.partial(strain_kernel, planes), name='strain', g...  4.44 us

profile of v2, /device:TPU:1, one launch (start us, length us, event | category | flops | bytes accessed | tf_op | source)
XLA Modules:
  0.0 75.3 jit_solution(8177098680684348051)
XLA Ops:
  0.6 0.0 copy-start
  0.6 1.4 %copy-done = f32[3,16,32,256]{3,2,1,0:T(8,128)S(1)} copy-done((f32[3,16,32,256]{3,2,1,0:T(8,128)S(1)}, f32[3,16,32,256]{3,2,1,0:T(8,128)}, u32[]{:S(2)}) %copy-start) | copy-done | bytes 1572888
  2.0 0.0 copy-start.1
  2.0 0.9 %copy-done.1 = bf16[256,3,128]{2,0,1:T(8,128)(2,1)S(1)} copy-done((bf16[256,3,128]{2,0,1:T(8,128)(2,1)S(1)}, bf16[256,3,128]{2,0,1:T(8,128)(2,1)}, u32[]{:S(2)}) %copy-start.1) | copy-done | bytes 196632
  3.0 0.0 copy-start.2
  3.0 0.8 %copy-done.2 = bf16[256,128]{1,0:T(8,128)(2,1)S(1)} copy-done((bf16[256,128]{1,0:T(8,128)(2,1)S(1)}, bf16[256,128]{1,0:T(8,128)(2,1)}, u32[]{:S(2)}) %copy-start.2) | copy-done | bytes 65560
  3.8 0.0 copy-start.3
  3.8 0.7 copy-done.3
  4.5 0.0 copy-start.4
  4.5 0.7 copy-done.4
  5.1 65.7 %wind_analysis.1 = (f32[3,18,32,256]{3,2,1,0:T(8,128)S(1)}, f32[2,32,128]{2,1,0:T(8,128)S(1)}, f32[1,128]{1,0:T(1,128)S(1)}) custom-call(s32[256]{0:T(256)S(1)} %copy-done.3, s32[1,128]{1,0:T(1,128)S(1)} %copy-done.4, f32[3,16,32,256]{3,2,1,0:T(8,128)S(1)} %copy-done, bf16[256,128,128]{2,1,0:T(8,128)(2,1)} %interp_hbm.1, bf16[3,256,128]{2,1,0:T(8,128)(2,1)S(1)} %bitcast.1, ...), custom_call_target="tpu_custom_call" | custom-call | tf_op jit(solution)/shard_map/wind_analysis/pallas_call | solution.py:460
  70.8 4.4 %strain.1 = (f32[3,16,32,256]{3,2,1,0:T(8,128)}, f32[6,16,32,256]{3,2,1,0:T(8,128)}, f32[2]{0:T(128)}) custom-call(f32[1,128]{1,0:T(1,128)S(1)} %get-tuple-element.6.cost_ref, f32[3,18,32,256]{3,2,1,0:T(8,128)S(1)} %get-tuple-element.7.wind_ref, f32[2,32,128]{2,1,0:T(8,128)S(1)} %get-tuple-element.8.edges_ref), custom_call_target="tpu_custom_call" | custom-call | tf_op jit(solution)/shard_map/strain/pallas_call | solution.py:498
Async XLA Ops:
  0.6 1.4 %copy-start = (f32[3,16,32,256]{3,2,1,0:T(8,128)S(1)}, f32[3,16,32,256]{3,2,1,0:T(8,128)}, u32[]{:S(2)}) copy-start(f32[3,16,32,256]{3,2,1,0:T(8,128)} %bg_hbm.1) | copy-start | bytes 4718596
  2.0 0.9 %copy-start.1 = (bf16[256,3,128]{2,0,1:T(8,128)(2,1)S(1)}, bf16[256,3,128]{2,0,1:T(8,128)(2,1)}, u32[]{:S(2)}) copy-start(bf16[256,3,128]{2,0,1:T(8,128)(2,1)} %param.8) | copy-start | bytes 589828
  3.0 0.8 %copy-start.2 = (bf16[256,128]{1,0:T(8,128)(2,1)S(1)}, bf16[256,128]{1,0:T(8,128)(2,1)}, u32[]{:S(2)}) copy-start(bf16[256,128]{1,0:T(8,128)(2,1)} %looked_hbm.1) | copy-start | bytes 196612
  3.8 0.7 copy-start.3
  4.5 0.7 copy-start.4

commit v3 on v2

v3 whole, which is shorter than its diff:
```python
import functools

import jax
import jax.numpy as jnp
from jax import lax
from jax.experimental import pallas as pl
from jax.experimental.pallas import tpu as pltpu
from jax.sharding import PartitionSpec as P

BACKGROUND_WEIGHT = 0.5
DIVERGENCE_WEIGHT = 1.0
STEP_LENGTH = 0.3
EPSILON = 1e-06
LANES = 128
F32 = jnp.float32
BF16 = jnp.bfloat16
LOGICAL = pl.DeviceIdType.LOGICAL
BACK, SPREAD0, GRAD0, SPREAD1, GRAD1, REST0 = range(6)


def iota(shape, dim):
    return lax.broadcasted_iota(jnp.int32, shape, dim)


def differences(nz, ny):
    sub = iota((nz, ny), 0)
    wide = iota((nz, ny), 1)

    def diff_z(v):
        up = jnp.where(sub == nz - 1, 0.0, pltpu.roll(v, nz - 1, 0))
        down = jnp.where(sub == 0, 0.0, pltpu.roll(v, 1, 0))
        return 0.5 * (up - down)

    def diff_y(v, low, high, x, k):
        at = 8 * x + k
        low = pltpu.roll(low, (LANES - at) % LANES if isinstance(at, int) else lax.rem(LANES - at, LANES), 1)
        high = pltpu.roll(high, LANES - 1 - at, 1)
        up = jnp.where(wide == ny - 1, jnp.concatenate([high] * (ny // LANES), 1), pltpu.roll(v, ny - 1, 1))
        down = jnp.where(wide == 0, jnp.concatenate([low] * (ny // LANES), 1), pltpu.roll(v, 1, 1))
        return 0.5 * (up - down)

    return diff_y, diff_z


def kernel(sizes, torus, block_hbm, count_hbm, bg_hbm, interp_hbm, beam_hbm, looked_hbm,
           wind_out, grad_out, info_out,
           weights, beams16, looked16, wind, grad0, grad1, spread0, spread1, push,
           block_ref, count_ref, codes_out, codes_in, out1, in1, out2, in2, out3, in3, out4, in4, out5, in5,
           info, pick, place, field, beams32, looked32, rays, looked, misfit0, held, edges_out, edges_in,
           send_sems, recv_sems, halo_send, halo_recv, local_sems):
    n_radar, n_tile, total_cells, total_gates = sizes
    n = n_radar * n_tile
    nx, nz, ny = wind.shape[1] - 2, wind.shape[2], wind.shape[3]
    half = nx * nz
    group = min(16, n // 2)
    r, t = lax.axis_index("radar"), lax.axis_index("tile")
    me = r * n_tile + t
    other = jnp.where(me + 1 >= n, me + 1 - n, me + 1)

    load_bg = pltpu.make_async_copy(bg_hbm, wind.at[:, pl.ds(1, nx)], local_sems.at[0])
    load_interp = pltpu.make_async_copy(interp_hbm, weights, local_sems.at[1])
    load_blocks = pltpu.make_async_copy(block_hbm, block_ref, local_sems.at[4])
    load_counts = pltpu.make_async_copy(count_hbm, count_ref, local_sems.at[5])
    load_beams = pltpu.make_async_copy(beam_hbm, beams16, local_sems.at[2])
    load_looked = pltpu.make_async_copy(looked_hbm, looked16, local_sems.at[3])
    load_blocks.start()
    load_counts.start()
    load_bg.start()
    load_beams.start()
    load_looked.start()
    load_interp.start()

    cores, ys, zs = torus
    xs = n_radar // cores
    rounds, turns = xs * ys, zs * cores

    def distance(i, size):
        if size == 1:
            return 0
        return jnp.where(i == size - 1, 0, jnp.where(i == 0, size // 2, i + lax.div(i, 2)))

    def round_base(i, sign):
        a, b = distance(lax.div(i, ys), xs), distance(lax.rem(i, ys), ys)
        x = lax.rem(lax.div(r, cores) + xs + sign * a, xs)
        y = lax.rem(lax.div(t, zs) + ys + sign * b, ys)
        return x * (cores * n_tile) + y * zs

    hops = sorted([(c, e) for c in range(zs) for e in range(cores)], key=lambda s: -min(s[0], zs - s[0]) - 0.5 * s[1])
    turn_base = {
        sign: [lax.rem(t + zs + sign * c, zs) + lax.rem(r + cores + sign * e, cores) * n_tile for c, e in hops]
        for sign in (1, -1)}

    def for_others(action):
        def one_round(i, carry):
            base = round_base(i, 1)
            for j in range(turns):
                action(i * turns + j, base + turn_base[1][j])
            return carry

        lax.fori_loop(0, rounds - 1, one_round, 0)
        base = round_base(rounds - 1, 1)
        for j in range(turns - 1):
            action((rounds - 1) * turns + j, base + turn_base[1][j])

    barrier = pltpu.get_barrier_semaphore()

    for_others(lambda k, d: pl.semaphore_signal(barrier, inc=1, device_id=d, device_id_type=LOGICAL))

    def over_planes(count, body, carry, at_once=2):
        def some(i, carry):
            stores = []
            for u in range(at_once):
                new, carry = body(i * at_once + u, carry)
                stores += new
            for ref, index, value in stores:
                ref[index] = value
            return carry

        return lax.fori_loop(0, count // at_once, some, carry)

    lane = iota((nz, LANES), 1)

    def pack_edges(stage, source, comps, one_field):
        def plane(x, carry):
            low, high = carry
            for k in range(comps):
                if one_field:
                    a, b = source[x + 1, :, :LANES], source[x + 1, :, ny - LANES :]
                else:
                    a, b = source[k, x + 1, :, :LANES], source[k, x + 1, :, ny - LANES :]
                to = 8 * x + k
                a = pltpu.roll(a, to, 1)
                b = pltpu.roll(b, to + 1, 1)
                low = jnp.where(lane == to, a, low)
                high = jnp.where(lane == to, b, high)
            return [], (low, high)

        zero = jnp.zeros((nz, LANES), F32)
        low, high = over_planes(nx, plane, (zero, zero), 4)
        edges_out[stage, 0] = low
        edges_out[stage, 1] = high

    def chosen_planes(array, x, part):
        if part == "one":
            return array.at[x]
        return array.at[{"all": pl.ds(0, 3), "first": pl.ds(0, 1), "rest": pl.ds(1, 2)}[part], x]

    def halo_copies(stage, array, part):
        def make(i, src, dst, device):
            return pltpu.make_async_remote_copy(
                src_ref=src, dst_ref=dst,
                send_sem=halo_send.at[stage, i], recv_sem=halo_recv.at[stage, i],
                device_id=device, device_id_type=LOGICAL)

        up_t = jnp.where(t < n_tile - 1, me + 1, me - 1)
        down_t = jnp.where(t > 0, me - 1, me + 1)
        up_r = jnp.where(r < n_radar - 1, me + n_tile, me - n_tile)
        down_r = jnp.where(r > 0, me - n_tile, me + n_tile)
        planes = functools.partial(chosen_planes, array, part=part)
        copies = [
            (t < n_tile - 1, t > 0, make(0, planes(nx), planes(0), up_t)),
            (t > 0, t < n_tile - 1, make(1, planes(1), planes(nx + 1), down_t)),
        ]
        if part != "rest":
            copies += [
                (r < n_radar - 1, r > 0, make(2, edges_out.at[stage, 1], edges_in.at[stage, 0], up_r)),
                (r > 0, r < n_radar - 1, make(3, edges_out.at[stage, 0], edges_in.at[stage, 1], down_r)),
            ]
        return copies

    def send_halos(stage, array, part="all"):
        for i, (sends, receives, copy) in enumerate(halo_copies(stage, array, part)):
            pl.when(sends)(copy.start)

            @pl.when(jnp.logical_not(receives))
            def _():
                if i >= 2:
                    edges_in[stage, i - 2] = jnp.zeros((nz, LANES), F32)
                else:
                    plane = chosen_planes(array, (nx + 1) * i, part)
                    plane[...] = jnp.zeros(plane.shape, F32)

    def await_halos(stage, array, part="all"):
        for sends, receives, copy in halo_copies(stage, array, part):
            pl.when(sends)(copy.wait_send)
            pl.when(receives)(copy.wait_recv)

    def exchange_copy(stage, src, dst, d, part):
        return pltpu.make_async_remote_copy(
            src_ref=src.at[d], dst_ref=dst.at[me],
            send_sem=send_sems.at[stage], recv_sem=recv_sems.at[stage, part],
            device_id=d, device_id_type=LOGICAL)

    def send_all(stage, src, dst, parts):
        for_others(lambda k, d: exchange_copy(stage, src, dst, d, k // group if parts else 0).start())
        dst[me] = src[me]

    def whole(stage, src, dst, part=0, count=n - 1):
        return pltpu.make_async_remote_copy(
            src_ref=src.at[pl.ds(0, count)], dst_ref=dst.at[pl.ds(0, count)],
            send_sem=send_sems.at[stage], recv_sem=recv_sems.at[stage, part],
            device_id=other, device_id_type=LOGICAL)

    diff_y, diff_z = differences(nz, ny)

    def divergence(stage, source, out):
        low, high = edges_in[stage, 0], edges_in[stage, 1]

        def plane(x, total):
            s = (0.5 * (source[0, x + 2] - source[0, x]) + diff_y(source[1, x + 1], low, high, x, 1)
                 + diff_z(source[2, x + 1]))
            return [(out, x + 1, s)], total + s * s

        return over_planes(nx, plane, jnp.zeros((nz, ny), F32))

    def pushes(stage, source, x, low, high):
        v = source[x + 1]
        return (0.5 * (source[x] - source[x + 2]), -diff_y(v, low, high, x, 0), -diff_z(v))

    def total_of(v):
        return jnp.sum(jnp.sum(v, axis=0, keepdims=True), axis=1, keepdims=True)

    def to_field(source):
        for h in range(ny // LANES):
            for k in range(3):
                v = source[k, 1 : nx + 1, :, h * LANES : (h + 1) * LANES]
                field[h * half : (h + 1) * half, k * LANES : (k + 1) * LANES] = v.reshape(half, LANES).astype(BF16)

    def gather(out, extra):
        chosen = jnp.dot(pick[...], field[...], preferred_element_type=F32)
        zero = jnp.zeros((n, LANES), F32)
        rows = []
        for k in range(2):
            for c in range(3):
                rows.append(chosen[k * n : (k + 1) * n, c * LANES : (c + 1) * LANES])
            rows.append(zero if k == 1 or extra is None else jnp.broadcast_to(extra, (n, LANES)))
        out[...] = jnp.swapaxes(jnp.stack(rows, 0), 0, 1).astype(BF16)

    def observe(source, out, dst, stage, step):
        count = n // group

        def members(q):
            bases = [round_base(q * (group // turns) + i, -1) for i in range(group // turns)]
            return [base + j for base in bases for j in turn_base[-1]]

        def weights_of(d):
            return weights[pl.ds(2 * d, 2)].reshape(2 * LANES, LANES)

        def project(ds):
            return [
                lax.dot_general(source[d], weights_of(d), (((1,), (1,)), ((), ())), preferred_element_type=F32)
                for d in ds]

        def adjoints(ds, projected, cost):
            beams = [rays[d] for d in ds]
            radial = [jnp.sum(b * p, axis=0, keepdims=True) for b, p in zip(beams, projected)]
            if step is None:
                misfit = [x - looked[d] for d, x in zip(ds, radial)]
                for d, x in zip(ds, misfit):
                    misfit0[d] = x
            else:
                misfit = [misfit0[d] - step * x for d, x in zip(ds, radial)]
            for x in misfit:
                cost = cost + x * x
            for u, (b, x) in enumerate(zip(beams, misfit)):
                held[u] = (b * x).astype(BF16)
            return cost

        def back(ds):
            return [jnp.dot(held[u], weights_of(d), preferred_element_type=F32) for u, d in enumerate(ds)]

        def send(ds, values, last):
            for d, x in zip(ds, values):
                out[d] = x.astype(BF16)
            for u, d in enumerate(ds):
                if last and u == group - 1:
                    dst[me] = out[me]
                else:
                    exchange_copy(stage, out, dst, d, 0).start()

        def arrive(q, last):
            if step is None:
                whole(stage - 1, out, source, q, group - last).wait_recv()

        def middle(q, cost, last=False):
            ds, ahead = members(q), members(q + 1)
            arrive(q + 1, last)
            values = back(ds)
            projected = project(ahead)
            send(ds, values, False)
            return adjoints(ahead, projected, cost)

        arrive(0, 0)
        first = members(0)
        cost = adjoints(first, project(first), jnp.zeros((1, 2 * LANES), F32))
        cost = lax.fori_loop(0, count - 2, middle, cost)
        cost = middle(count - 2, cost, True)
        final = members(count - 1)
        send(final, back(final), True)
        return 0.5 * jnp.sum(cost, axis=1, keepdims=True)

    def scatter(source, out, to_field):
        rows = jnp.swapaxes(source[...].astype(F32), 0, 1).astype(BF16)
        landed = jnp.concatenate(
            [jnp.concatenate([rows[4 * k + c] for c in range(3)], 1) for k in range(2)], 0)
        total = jnp.zeros((nz, LANES), F32)
        for h in range(ny // LANES):
            added = jnp.dot(place[h * half : (h + 1) * half], landed, preferred_element_type=F32)
            for c in range(3):
                lanes = slice(h * LANES, (h + 1) * LANES)
                v = added[:, c * LANES : (c + 1) * LANES].reshape(nx, nz, LANES) + push[c, :, :, lanes]
                out[c, 1 : nx + 1, :, lanes] = v
                total = total + jnp.sum(v * v, axis=0)
                if to_field:
                    field[h * half : (h + 1) * half, c * LANES : (c + 1) * LANES] = v.reshape(half, LANES).astype(BF16)
        return total_of(total)

    ahead = iota((1, LANES), 1) < LANES // 2

    def code_rows(q, carry):
        ds = [q * 8 + u for u in range(8)]
        counts = [count_ref[0, d] for d in ds]
        blocks = [[block_ref[0, 2 * d + k] for k in range(2)] for d in ds]
        rows = []
        for count, pair in zip(counts, blocks):
            codes = [lax.rem(b, ny // LANES) * half + lax.div(b, ny // LANES) for b in pair]
            codes = [jnp.where(k < count, c, -1) for k, c in enumerate(codes)]
            rows.append(jnp.where(ahead, codes[0], codes[1]))
        for d, row in zip(ds, rows):
            codes_out[d] = row
        return carry

    load_blocks.wait()
    load_counts.wait()
    lax.fori_loop(0, n // 8, code_rows, 0)
    load_bg.wait()
    pack_edges(BACK, wind, 3, False)
    pl.semaphore_wait(barrier, n - 1)
    send_all(0, codes_out, codes_in, False)
    send_halos(BACK, wind)
    to_field(wind)

    load_beams.wait()
    load_looked.wait()
    beams32[...] = beams16[...].astype(F32)
    looked32[...] = looked16[...].astype(F32)
    zero = jnp.zeros((n, LANES), F32)
    rows = []
    for k in range(2):
        rows += [beams32[c, pl.ds(k, n, stride=2), :] for c in range(3)] + [zero]
    out_row = jnp.swapaxes(jnp.stack(rows, 0), 0, 1)
    rays[:, :, :LANES] = out_row
    eight = iota((8, LANES), 0)

    def ray_rows(q, carry):
        ds = [q * 8 + u for u in range(8)]
        counts = [count_ref[0, d] for d in ds]
        values = [rays[d, :, :LANES] for d in ds]
        seen = [[looked32[pl.ds(2 * d + k, 1), :] for k in range(2)] for d in ds]
        for d, count, v, s in zip(ds, counts, values, seen):
            rays[d, :, :LANES] = jnp.where((eight < 4) & (count > 0), v, 0.0)
            rays[d, :, LANES:] = jnp.where((eight >= 4) & (count > 1), v, 0.0)
            looked[d] = jnp.concatenate([jnp.where(count > k, s[k], 0.0) for k in range(2)], 1)
        return carry

    lax.fori_loop(0, n // 8, ray_rows, 0)

    whole(0, codes_out, codes_in).wait_recv()
    codes = codes_in[...].reshape(n, LANES)
    turned = pltpu.roll(codes, LANES // 2, 1)
    front = iota((n, LANES), 1) < LANES // 2
    code = (jnp.where(front, codes, turned), jnp.where(front, turned, codes))
    for k in range(2):
        for j in range(pick.shape[1] // LANES):
            hit = code[k] == iota((n, LANES), 1) + j * LANES
            pick[k * n : (k + 1) * n, j * LANES : (j + 1) * LANES] = jnp.where(hit, 1.0, 0.0).astype(BF16)

    gather(out1, None)
    send_all(1, out1, in1, True)
    for k in range(2):
        across = jnp.transpose(code[k])
        for j in range(pick.shape[1] // LANES):
            hit = across == iota((LANES, n), 0) + j * LANES
            place[j * LANES : (j + 1) * LANES, k * n : (k + 1) * n] = jnp.where(hit, 1.0, 0.0).astype(BF16)
    await_halos(BACK, wind)
    spread_cost0 = 0.5 * DIVERGENCE_WEIGHT * total_of(divergence(BACK, wind, spread0))
    pack_edges(SPREAD0, spread0, 1, True)
    send_halos(SPREAD0, spread0, "one")
    load_interp.wait()
    cost0 = observe(in1, out2, in2, 2, None) + spread_cost0
    await_halos(SPREAD0, spread0, "one")
    low, high = edges_in[SPREAD0, 0], edges_in[SPREAD0, 1]

    def push_plane(x, carry):
        values = pushes(SPREAD0, spread0, x, low, high)
        return [(push, (c, x), DIVERGENCE_WEIGHT * v) for c, v in enumerate(values)], carry

    over_planes(nx, push_plane, 0)
    whole(2, out2, in2).wait_recv()
    squares = scatter(in2, grad0, True)

    first = squares.astype(BF16)
    rest = squares - first.astype(F32)
    second = rest.astype(BF16)
    third = (rest - second.astype(F32)).astype(BF16)
    at = iota((1, LANES), 1)
    extra = jnp.where(at == 0, first.astype(F32), jnp.where(at == 1, second.astype(F32), jnp.where(at == 2, third.astype(F32), 0.0)))
    gather(out3, extra)
    pack_edges(GRAD0, grad0, 3, False)
    send_halos(GRAD0, grad0, "first")
    send_all(3, out3, in3, False)
    await_halos(GRAD0, grad0, "first")
    divergence(GRAD0, grad0, spread1)
    pack_edges(SPREAD1, spread1, 1, True)
    send_halos(SPREAD1, spread1, "one")
    whole(3, out3, in3).wait_recv()
    squares = jnp.sum(jnp.sum(in3[...].astype(F32), axis=0)[3:4], axis=1, keepdims=True)
    step0 = STEP_LENGTH / jnp.sqrt(squares / total_cells + EPSILON)
    cost1 = observe(in3, out4, in4, 4, step0)

    def wind_plane(x, carry):
        return [(wind, (c, x), wind[c, x] - step0 * grad0[c, x]) for c in range(3)], carry

    send_halos(REST0, grad0, "rest")
    await_halos(SPREAD1, spread1, "one")
    low1, high1 = edges_in[SPREAD1, 0], edges_in[SPREAD1, 1]

    def update_plane(x, carry):
        offsets, spreads = carry
        stores = []
        for c, v in enumerate(pushes(SPREAD1, spread1, x, low1, high1)):
            offset = -step0 * grad0[c, x + 1]
            offsets = offsets + offset * offset
            stores.append((push, (c, x), push[c, x] - step0 * (DIVERGENCE_WEIGHT * v) + BACKGROUND_WEIGHT * offset))
        spread = spread0[x + 1] - step0 * spread1[x + 1]
        return stores, (offsets, spreads + spread * spread)

    zero = jnp.zeros((nz, ny), F32)
    offsets, spreads = over_planes(nx, update_plane, (zero, zero))
    cost1 = cost1 + 0.5 * total_of(BACKGROUND_WEIGHT * offsets + DIVERGENCE_WEIGHT * spreads)
    await_halos(REST0, grad0, "rest")
    over_planes(nx + 2, wind_plane, 0)
    save_wind = pltpu.make_async_copy(wind, wind_out, local_sems.at[6])
    save_wind.start()
    whole(4, out4, in4).wait_recv()
    squares = scatter(in4, grad1, False)

    inner = pl.ds(1, nx)
    save_grad = pltpu.make_async_copy(grad1.at[:, inner], grad_out.at[:, inner], local_sems.at[7])
    summary = jnp.where(at == 0, squares, jnp.where(at == 1, cost0, jnp.where(at == 2, cost1, 0.0)))

    out5[...] = summary

    for_others(lambda k, d: pltpu.make_async_remote_copy(
        src_ref=out5, dst_ref=in5.at[me], send_sem=send_sems.at[5], recv_sem=recv_sems.at[5, 0],
        device_id=d, device_id_type=LOGICAL).start())
    in5[me] = summary
    save_grad.start()
    pack_edges(GRAD1, grad1, 3, False)
    send_halos(GRAD1, grad1)
    for i in range(2):
        info[i] = edges_in[BACK, i] - step0 * edges_in[GRAD0, i]
    info[4] = jnp.zeros((nz, LANES), F32)
    await_halos(GRAD1, grad1)
    for i in range(2):
        info[2 + i] = edges_in[GRAD1, i]
    save_edges = [
        pltpu.make_async_copy(grad1.at[:, x], grad_out.at[:, x], local_sems.at[9 + i])
        for i, x in enumerate((0, nx + 1))]
    for copy in save_edges:
        copy.start()
    whole(5, in5, in5).wait_recv()
    sums = jnp.sum(in5[...], axis=0)
    squares = jnp.sum(jnp.where(at == 0, sums, 0.0), axis=1, keepdims=True)
    step1 = STEP_LENGTH / jnp.sqrt(squares / total_cells + EPSILON)
    info[4, 0:1, :] = jnp.where(at == 0, step1, sums / total_gates)
    save_info = pltpu.make_async_copy(info, info_out, local_sems.at[8])
    save_info.start()
    save_info.wait()
    for copy in save_edges:
        copy.wait()
    save_grad.wait()
    save_wind.wait()

    pairs = ((codes_out, codes_in), (out1, in1), (out2, in2), (out3, in3), (out4, in4), (in5, in5))
    for stage, (src, dst) in enumerate(pairs):
        whole(stage, src, dst).wait_send()


def strain_kernel(wind_hbm, grad_hbm, info_hbm, final_hbm, strain_hbm, trace_ref,
                  wind, grad, info, strain, wind_sems, grad_sems, info_sem, final_sems, strain_sems):
    nx, nz, ny = wind.shape[1] - 2, wind.shape[2], wind.shape[3]
    diff_y, diff_z = differences(nz, ny)
    load_info = pltpu.make_async_copy(info_hbm, info, info_sem)
    load_info.start()
    starts = list(range(0, nx + 2, 4))
    loads = []
    for i, start in enumerate(starts):
        span = pl.ds(start, min(4, nx + 2 - start))
        loads.append((
            pltpu.make_async_copy(wind_hbm.at[:, span], wind.at[:, span], wind_sems.at[i]),
            pltpu.make_async_copy(grad_hbm.at[:, span], grad.at[:, span], grad_sems.at[i])))
        for copy in loads[-1]:
            copy.start()
    load_info.wait()
    step = info[4, 0:1, 0:1]
    low, high = (info[i] - step * info[2 + i] for i in range(2))
    scalars = info[4, 0:1, :]
    at = iota((1, LANES), 1)
    for i in range(2):
        trace_ref[i] = jnp.sum(jnp.where(at == i + 1, scalars, 0.0))

    ready, saves = 0, []
    for j in range(nx // 2):
        while ready < len(starts) and starts[ready] <= 2 * j + 3:
            for copy in loads[ready]:
                copy.wait()
            for x in range(starts[ready], min(starts[ready] + 4, nx + 2)):
                new = [wind[c, x] - step * grad[c, x] for c in range(3)]
                for c in range(3):
                    wind[c, x] = new[c]
            ready += 1
        stores = []
        for x in (2 * j, 2 * j + 1):
            v = [wind[c, x + 1] for c in range(3)]
            dx = [0.5 * (wind[c, x + 2] - wind[c, x]) for c in range(3)]
            dy = [diff_y(v[c], low, high, x, c) for c in range(3)]
            dz = [diff_z(v[c]) for c in range(3)]
            values = (dx[0], dy[1], dz[2], 0.5 * (dy[0] + dx[1]), 0.5 * (dz[0] + dx[2]), 0.5 * (dz[1] + dy[2]))
            stores += [(c, x, value) for c, value in enumerate(values)]
        for c, x, value in stores:
            strain[c, x] = value
        pair = pl.ds(2 * j, 2)
        saves += [
            pltpu.make_async_copy(wind.at[:, pl.ds(2 * j + 1, 2)], final_hbm.at[:, pair], final_sems.at[j]),
            pltpu.make_async_copy(strain.at[:, pair], strain_hbm.at[:, pair], strain_sems.at[j])]
        for copy in saves[-2:]:
            copy.start()
    for copy in saves:
        copy.wait()


def shards(n_radar, n_tile, background, interp, beam, observed, cell_block, sweep_count):
    n = n_radar * n_tile
    _, nx, nz, ny = background.shape
    slots = interp.shape[0] // n
    gate = interp.shape[1]
    blocks = nx * nz * ny // gate
    total_cells = 3 * nx * nz * ny * n
    total_gates = interp.shape[0] * n * gate
    sizes = (n_radar, n_tile, total_cells, total_gates)
    torus = (2, n_tile // 4, 4)

    smem = pl.BlockSpec(memory_space=pltpu.SMEM)
    hbm = pl.BlockSpec(memory_space=pltpu.HBM)
    message = pltpu.VMEM((n, 8, LANES), BF16)
    row = pltpu.VMEM((n, 1, LANES), F32)
    code_row = pltpu.VMEM((n, 1, LANES), jnp.int32)
    padded = pltpu.VMEM((3, nx + 2, nz, ny), F32)
    single = pltpu.VMEM((nx + 2, nz, ny), F32)
    rays = jnp.transpose(beam, (1, 0, 2))
    groups = n // min(16, n // 2)
    wind, grad, info = pl.pallas_call(
        functools.partial(kernel, sizes, torus),
        name="wind_analysis",
        out_shape=(
            jax.ShapeDtypeStruct((3, nx + 2, nz, ny), F32),
            jax.ShapeDtypeStruct((3, nx + 2, nz, ny), F32),
            jax.ShapeDtypeStruct((5, nz, LANES), F32),
        ),
        in_specs=[hbm] * 6,
        out_specs=(hbm, hbm, hbm),
        scratch_shapes=[
            pltpu.VMEM(interp.shape, BF16),
            pltpu.VMEM(rays.shape, BF16),
            pltpu.VMEM(observed.shape, BF16),
            padded, padded, padded, single, single,
            pltpu.VMEM((3, nx, nz, ny), F32),
            pltpu.SMEM((1, n * slots), jnp.int32), pltpu.SMEM((1, n), jnp.int32),
            code_row, code_row, message, message, message, message, message, message, message, message, pltpu.VMEM((1, LANES), F32), row,
            pltpu.VMEM((5, nz, LANES), F32),
            pltpu.VMEM((slots * n, blocks), BF16),
            pltpu.VMEM((blocks, slots * n), BF16),
            pltpu.VMEM((blocks, 3 * LANES), BF16),
            pltpu.VMEM(rays.shape, F32),
            pltpu.VMEM(observed.shape, F32),
            pltpu.VMEM((n, 8, slots * gate), F32),
            pltpu.VMEM((n, 1, slots * gate), F32),
            pltpu.VMEM((n, 1, slots * gate), F32),
            pltpu.VMEM((n // groups, 8, slots * gate), BF16),
            pltpu.VMEM((5, 2, nz, LANES), F32),
            pltpu.VMEM((5, 2, nz, LANES), F32),
            pltpu.SemaphoreType.DMA((6,)),
            pltpu.SemaphoreType.DMA((6, groups)),
            pltpu.SemaphoreType.DMA((6, 4)),
            pltpu.SemaphoreType.DMA((6, 4)),
            pltpu.SemaphoreType.DMA((11,)),
        ],
        compiler_params=pltpu.CompilerParams(
            collective_id=0, has_side_effects=True, vmem_limit_bytes=60 * 2**20),
    )(cell_block.reshape(1, n * slots), sweep_count, background, interp, rays, observed)

    spans = len(range(0, nx + 2, 4))
    return pl.pallas_call(
        strain_kernel,
        name="strain",
        out_shape=(
            jax.ShapeDtypeStruct(background.shape, F32),
            jax.ShapeDtypeStruct((6, nx, nz, ny), F32),
            jax.ShapeDtypeStruct((2,), F32),
        ),
        in_specs=[hbm] * 3,
        out_specs=(hbm, hbm, smem),
        scratch_shapes=[
            padded, padded, pltpu.VMEM((5, nz, LANES), F32), pltpu.VMEM((6, nx, nz, ny), F32),
            pltpu.SemaphoreType.DMA((spans,)), pltpu.SemaphoreType.DMA((spans,)), pltpu.SemaphoreType.DMA,
            pltpu.SemaphoreType.DMA((nx // 2,)), pltpu.SemaphoreType.DMA((nx // 2,))],
        compiler_params=pltpu.CompilerParams(vmem_limit_bytes=60 * 2**20),
    )(wind, grad, info)


def solution(mesh):
    n_radar, n_tile = mesh.shape["radar"], mesh.shape["tile"]
    both = ("radar", "tile")
    in_specs = (
        P(None, "tile", None, "radar"), P(both, None, None), P(both, None, None),
        P(both, None), P(both), P(both, None))
    out_specs = (P(None, "tile", None, "radar"), P(None, "tile", None, "radar"), P())
    return jax.shard_map(
        functools.partial(shards, n_radar, n_tile), mesh=mesh, in_specs=in_specs, out_specs=out_specs, check_vma=False)
```

time: 75.5 us -> 65.2 us (0.86)
  Pallas kernels: 70.1 us -> 64.4 us
  local copies, waits for them, and re-layouts: 4.5 us -> 0 us
    pallas_call x2, Pallas kernels: 70.1 us -> 64.4 us  [the longest x1 59.3 us: shards(): pl.pallas_call(functools.partial(kernel, sizes, torus), name='wind_analys...]
    unnamed x10 -> x0, local copies, waits for them, and re-layouts: 4.5 us -> none
where the time goes in v3:
time: 65.2 us; the launch traced here: 65.1 us
  Pallas kernels  64.4 us (99%)
    pallas_call x1, Pallas kernels, shards(): pl.pallas_call(functools.partial(kernel, sizes, torus), name='wind_analys...  59.3 us
    pallas_call x1, Pallas kernels, shards(): pl.pallas_call(strain_kernel, name='strain', out_shape=(jax.ShapeDtypeStr...  5.13 us

profile of v3, /device:TPU:1, one launch (start us, length us, event | category | flops | bytes accessed | tf_op | source)
XLA Modules:
  0.0 65.1 jit_solution(11266076430701137326)
XLA Ops:
  0.6 59.3 %wind_analysis.1 = (f32[3,18,32,256]{3,2,1,0:T(8,128)}, f32[3,18,32,256]{3,2,1,0:T(8,128)}, f32[5,32,128]{2,1,0:T(8,128)}) custom-call(s32[1,256]{1,0:T(1,128)} %bitcast.3, s32[1,128]{1,0:T(1,128)} %count_hbm.1, f32[3,16,32,256]{3,2,1,0:T(8,128)} %bg_hbm.1, bf16[256,128,128]{2,1,0:T(8,128)(2,1)} %interp_hbm.1, bf16[3,256,128]{2,1,0:T(8,128)(2,1)} %bitcast.2, ...), custom_call_target="tpu_custom_call" | custom-call | tf_op jit(solution)/shard_map/wind_analysis/pallas_call | solution.py:563
  59.9 5.1 %strain.1 = (f32[3,16,32,256]{3,2,1,0:T(8,128)}, f32[6,16,32,256]{3,2,1,0:T(8,128)}, f32[2]{0:T(128)}) custom-call(f32[3,18,32,256]{3,2,1,0:T(8,128)} %get-tuple-element.6.wind_hbm, f32[3,18,32,256]{3,2,1,0:T(8,128)} %get-tuple-element.7.grad_hbm, f32[5,32,128]{2,1,0:T(8,128)} %get-tuple-element.8.info_hbm), custom_call_target="tpu_custom_call" | custom-call | tf_op jit(solution)/shard_map/strain/pallas_call | solution.py:604

commit v4 on v3

--- a/solution.py
+++ b/solution.py
@@ -185,9 +185,12 @@
             pl.when(sends)(copy.wait_send)
             pl.when(receives)(copy.wait_recv)
 
+    def used(stage, ref, span):
+        return ref.at[span, pl.ds(0, 6)] if stage in (1, 2, 4) else ref.at[span]
+
     def exchange_copy(stage, src, dst, d, part):
         return pltpu.make_async_remote_copy(
-            src_ref=src.at[d], dst_ref=dst.at[me],
+            src_ref=used(stage, src, d), dst_ref=used(stage, dst, me),
             send_sem=send_sems.at[stage], recv_sem=recv_sems.at[stage, part],
             device_id=d, device_id_type=LOGICAL)
 
@@ -197,7 +200,7 @@
 
     def whole(stage, src, dst, part=0, count=n - 1):
         return pltpu.make_async_remote_copy(
-            src_ref=src.at[pl.ds(0, count)], dst_ref=dst.at[pl.ds(0, count)],
+            src_ref=used(stage, src, pl.ds(0, count)), dst_ref=used(stage, dst, pl.ds(0, count)),
             send_sem=send_sems.at[stage], recv_sem=recv_sems.at[stage, part],
             device_id=other, device_id_type=LOGICAL)
 
@@ -233,7 +236,7 @@
         for k in range(2):
             for c in range(3):
                 rows.append(chosen[k * n : (k + 1) * n, c * LANES : (c + 1) * LANES])
-            rows.append(zero if k == 1 or extra is None else jnp.broadcast_to(extra, (n, LANES)))
+        rows += [zero if extra is None else jnp.broadcast_to(extra, (n, LANES)), zero]
         out[...] = jnp.swapaxes(jnp.stack(rows, 0), 0, 1).astype(BF16)
 
     def observe(source, out, dst, stage, step):
@@ -302,7 +305,7 @@
     def scatter(source, out, to_field):
         rows = jnp.swapaxes(source[...].astype(F32), 0, 1).astype(BF16)
         landed = jnp.concatenate(
-            [jnp.concatenate([rows[4 * k + c] for c in range(3)], 1) for k in range(2)], 0)
+            [jnp.concatenate([rows[3 * k + c] for c in range(3)], 1) for k in range(2)], 0)
         total = jnp.zeros((nz, LANES), F32)
         for h in range(ny // LANES):
             added = jnp.dot(place[h * half : (h + 1) * half], landed, preferred_element_type=F32)
@@ -330,6 +333,7 @@
             codes_out[d] = row
         return carry
 
+    in1[:, 6:, :] = jnp.zeros((n, 2, LANES), BF16)
     load_blocks.wait()
     load_counts.wait()
     lax.fori_loop(0, n // 8, code_rows, 0)
@@ -347,7 +351,8 @@
     zero = jnp.zeros((n, LANES), F32)
     rows = []
     for k in range(2):
-        rows += [beams32[c, pl.ds(k, n, stride=2), :] for c in range(3)] + [zero]
+        rows += [beams32[c, pl.ds(k, n, stride=2), :] for c in range(3)]
+    rows += [zero, zero]
     out_row = jnp.swapaxes(jnp.stack(rows, 0), 0, 1)
     rays[:, :, :LANES] = out_row
     eight = iota((8, LANES), 0)
@@ -358,8 +363,8 @@
         values = [rays[d, :, :LANES] for d in ds]
         seen = [[looked32[pl.ds(2 * d + k, 1), :] for k in range(2)] for d in ds]
         for d, count, v, s in zip(ds, counts, values, seen):
-            rays[d, :, :LANES] = jnp.where((eight < 4) & (count > 0), v, 0.0)
-            rays[d, :, LANES:] = jnp.where((eight >= 4) & (count > 1), v, 0.0)
+            rays[d, :, :LANES] = jnp.where((eight < 3) & (count > 0), v, 0.0)
+            rays[d, :, LANES:] = jnp.where((eight >= 3) & (count > 1), v, 0.0)
             looked[d] = jnp.concatenate([jnp.where(count > k, s[k], 0.0) for k in range(2)], 1)
         return carry
 
@@ -414,7 +419,7 @@
     pack_edges(SPREAD1, spread1, 1, True)
     send_halos(SPREAD1, spread1, "one")
     whole(3, out3, in3).wait_recv()
-    squares = jnp.sum(jnp.sum(in3[...].astype(F32), axis=0)[3:4], axis=1, keepdims=True)
+    squares = jnp.sum(jnp.sum(in3[...].astype(F32), axis=0)[6:7], axis=1, keepdims=True)
     step0 = STEP_LENGTH / jnp.sqrt(squares / total_cells + EPSILON)
     cost1 = observe(in3, out4, in4, 4, step0)
 
@@ -438,10 +443,6 @@
     zero = jnp.zeros((nz, ny), F32)
     offsets, spreads = over_planes(nx, update_plane, (zero, zero))
     cost1 = cost1 + 0.5 * total_of(BACKGROUND_WEIGHT * offsets + DIVERGENCE_WEIGHT * spreads)
-    await_halos(REST0, grad0, "rest")
-    over_planes(nx + 2, wind_plane, 0)
-    save_wind = pltpu.make_async_copy(wind, wind_out, local_sems.at[6])
-    save_wind.start()
     whole(4, out4, in4).wait_recv()
     squares = scatter(in4, grad1, False)
 
@@ -458,6 +459,10 @@
     save_grad.start()
     pack_edges(GRAD1, grad1, 3, False)
     send_halos(GRAD1, grad1)
+    await_halos(REST0, grad0, "rest")
+    over_planes(nx + 2, wind_plane, 0)
+    save_wind = pltpu.make_async_copy(wind, wind_out, local_sems.at[6])
+    save_wind.start()
     for i in range(2):
         info[i] = edges_in[BACK, i] - step0 * edges_in[GRAD0, i]
     info[4] = jnp.zeros((nz, LANES), F32)

time: 65.2 us -> 64 us (0.982)
  Pallas kernels: 64.4 us -> 63.2 us
    pallas_call x1, Pallas kernels: 59.3 us -> 58.1 us  [shards(): pl.pallas_call(functools.partial(kernel, sizes, torus), name='wind_analys...]
where the time goes in v4:
time: 64 us; the launch traced here: 63.9 us
  Pallas kernels  63.2 us (99%)
  between operations  0.64 us (1%)
    pallas_call x1, Pallas kernels, shards(): pl.pallas_call(functools.partial(kernel, sizes, torus), name='wind_analys...  58.1 us
    pallas_call x1, Pallas kernels, shards(): pl.pallas_call(strain_kernel, name='strain', out_shape=(jax.ShapeDtypeStr...  5.13 us

profile of v4, /device:TPU:1, one launch (start us, length us, event | category | flops | bytes accessed | tf_op | source)
XLA Modules:
  0.0 63.9 jit_solution(6188591726379337789)
XLA Ops:
  0.6 58.1 %wind_analysis.1 = (f32[3,18,32,256]{3,2,1,0:T(8,128)}, f32[3,18,32,256]{3,2,1,0:T(8,128)}, f32[5,32,128]{2,1,0:T(8,128)}) custom-call(s32[1,256]{1,0:T(1,128)} %bitcast.3, s32[1,128]{1,0:T(1,128)} %count_hbm.1, f32[3,16,32,256]{3,2,1,0:T(8,128)} %bg_hbm.1, bf16[256,128,128]{2,1,0:T(8,128)(2,1)} %interp_hbm.1, bf16[3,256,128]{2,1,0:T(8,128)(2,1)} %bitcast.2, ...), custom_call_target="tpu_custom_call" | custom-call | tf_op jit(solution)/shard_map/wind_analysis/pallas_call | solution.py:568
  58.7 5.1 %strain.1 = (f32[3,16,32,256]{3,2,1,0:T(8,128)}, f32[6,16,32,256]{3,2,1,0:T(8,128)}, f32[2]{0:T(128)}) custom-call(f32[3,18,32,256]{3,2,1,0:T(8,128)} %get-tuple-element.6.wind_hbm, f32[3,18,32,256]{3,2,1,0:T(8,128)} %get-tuple-element.7.grad_hbm, f32[5,32,128]{2,1,0:T(8,128)} %get-tuple-element.8.info_hbm), custom_call_target="tpu_custom_call" | custom-call | tf_op jit(solution)/shard_map/strain/pallas_call | solution.py:609

commit v5 on v4

--- a/solution.py
+++ b/solution.py
@@ -72,39 +72,35 @@
 
     cores, ys, zs = torus
     xs = n_radar // cores
-    rounds, turns = xs * ys, zs * cores
+    turns = zs * cores
 
     def distance(i, size):
         if size == 1:
             return 0
         return jnp.where(i == size - 1, 0, jnp.where(i == 0, size // 2, i + lax.div(i, 2)))
 
-    def round_base(i, sign):
+    def round_base(i):
         a, b = distance(lax.div(i, ys), xs), distance(lax.rem(i, ys), ys)
-        x = lax.rem(lax.div(r, cores) + xs + sign * a, xs)
-        y = lax.rem(lax.div(t, zs) + ys + sign * b, ys)
+        x = lax.rem(lax.div(r, cores) + a, xs)
+        y = lax.rem(lax.div(t, zs) + b, ys)
         return x * (cores * n_tile) + y * zs
 
     hops = sorted([(c, e) for c in range(zs) for e in range(cores)], key=lambda s: -min(s[0], zs - s[0]) - 0.5 * s[1])
-    turn_base = {
-        sign: [lax.rem(t + zs + sign * c, zs) + lax.rem(r + cores + sign * e, cores) * n_tile for c, e in hops]
-        for sign in (1, -1)}
+    turn_base = [lax.rem(t + c, zs) + lax.rem(r + e, cores) * n_tile for c, e in hops]
+    x_base = [lax.rem(lax.div(r, cores) + i, xs) * (cores * n_tile) for i in range(xs)]
+    y_base = [lax.rem(lax.div(t, zs) + i, ys) * zs for i in range(ys)]
+    z_base = [lax.rem(t + i, zs) for i in range(zs)]
+    core_base = [lax.rem(r + i, cores) * n_tile for i in range(cores)]
+    trips = [(a, b, c, e) for a in range(xs) for b in range(ys) for c in range(zs) for e in range(cores)]
+    trips.sort(key=lambda s: -min(s[0], xs - s[0]) - min(s[1], ys - s[1]) - min(s[2], zs - s[2]) - 0.5 * s[3])
 
     def for_others(action):
-        def one_round(i, carry):
-            base = round_base(i, 1)
-            for j in range(turns):
-                action(i * turns + j, base + turn_base[1][j])
-            return carry
-
-        lax.fori_loop(0, rounds - 1, one_round, 0)
-        base = round_base(rounds - 1, 1)
-        for j in range(turns - 1):
-            action((rounds - 1) * turns + j, base + turn_base[1][j])
+        for a, b, c, e in trips[:-1]:
+            action(x_base[a] + y_base[b] + z_base[c] + core_base[e])
 
     barrier = pltpu.get_barrier_semaphore()
 
-    for_others(lambda k, d: pl.semaphore_signal(barrier, inc=1, device_id=d, device_id_type=LOGICAL))
+    for_others(lambda d: pl.semaphore_signal(barrier, inc=1, device_id=d, device_id_type=LOGICAL))
 
     def over_planes(count, body, carry, at_once=2):
         def some(i, carry):
@@ -188,20 +184,21 @@
     def used(stage, ref, span):
         return ref.at[span, pl.ds(0, 6)] if stage in (1, 2, 4) else ref.at[span]
 
-    def exchange_copy(stage, src, dst, d, part):
+    def exchange_copy(stage, src, dst, d):
         return pltpu.make_async_remote_copy(
             src_ref=used(stage, src, d), dst_ref=used(stage, dst, me),
-            send_sem=send_sems.at[stage], recv_sem=recv_sems.at[stage, part],
+            send_sem=send_sems.at[stage], recv_sem=recv_sems.at[stage],
             device_id=d, device_id_type=LOGICAL)
 
-    def send_all(stage, src, dst, parts):
-        for_others(lambda k, d: exchange_copy(stage, src, dst, d, k // group if parts else 0).start())
+    def send_all(stage, src, dst):
+        for_others(lambda d: exchange_copy(stage, src, dst, d).start())
         dst[me] = src[me]
 
-    def whole(stage, src, dst, part=0, count=n - 1):
+    def whole(stage, src, dst):
+        count = n - 1
         return pltpu.make_async_remote_copy(
             src_ref=used(stage, src, pl.ds(0, count)), dst_ref=used(stage, dst, pl.ds(0, count)),
-            send_sem=send_sems.at[stage], recv_sem=recv_sems.at[stage, part],
+            send_sem=send_sems.at[stage], recv_sem=recv_sems.at[stage],
             device_id=other, device_id_type=LOGICAL)
 
     diff_y, diff_z = differences(nz, ny)
@@ -243,8 +240,8 @@
         count = n // group
 
         def members(q):
-            bases = [round_base(q * (group // turns) + i, -1) for i in range(group // turns)]
-            return [base + j for base in bases for j in turn_base[-1]]
+            bases = [round_base(q * (group // turns) + i) for i in range(group // turns)]
+            return [base + j for base in bases for j in turn_base]
 
         def weights_of(d):
             return weights[pl.ds(2 * d, 2)].reshape(2 * LANES, LANES)
@@ -279,25 +276,18 @@
                 if last and u == group - 1:
                     dst[me] = out[me]
                 else:
-                    exchange_copy(stage, out, dst, d, 0).start()
-
-        def arrive(q, last):
-            if step is None:
-                whole(stage - 1, out, source, q, group - last).wait_recv()
-
-        def middle(q, cost, last=False):
+                    exchange_copy(stage, out, dst, d).start()
+
+        def middle(q, cost):
             ds, ahead = members(q), members(q + 1)
-            arrive(q + 1, last)
             values = back(ds)
             projected = project(ahead)
             send(ds, values, False)
             return adjoints(ahead, projected, cost)
 
-        arrive(0, 0)
         first = members(0)
         cost = adjoints(first, project(first), jnp.zeros((1, 2 * LANES), F32))
-        cost = lax.fori_loop(0, count - 2, middle, cost)
-        cost = middle(count - 2, cost, True)
+        cost = lax.fori_loop(0, count - 1, middle, cost)
         final = members(count - 1)
         send(final, back(final), True)
         return 0.5 * jnp.sum(cost, axis=1, keepdims=True)
@@ -340,7 +330,7 @@
     load_bg.wait()
     pack_edges(BACK, wind, 3, False)
     pl.semaphore_wait(barrier, n - 1)
-    send_all(0, codes_out, codes_in, False)
+    send_all(0, codes_out, codes_in)
     send_halos(BACK, wind)
     to_field(wind)
 
@@ -381,7 +371,7 @@
             pick[k * n : (k + 1) * n, j * LANES : (j + 1) * LANES] = jnp.where(hit, 1.0, 0.0).astype(BF16)
 
     gather(out1, None)
-    send_all(1, out1, in1, True)
+    send_all(1, out1, in1)
     for k in range(2):
         across = jnp.transpose(code[k])
         for j in range(pick.shape[1] // LANES):
@@ -392,6 +382,7 @@
     pack_edges(SPREAD0, spread0, 1, True)
     send_halos(SPREAD0, spread0, "one")
     load_interp.wait()
+    whole(1, out1, in1).wait_recv()
     cost0 = observe(in1, out2, in2, 2, None) + spread_cost0
     await_halos(SPREAD0, spread0, "one")
     low, high = edges_in[SPREAD0, 0], edges_in[SPREAD0, 1]
@@ -413,7 +404,7 @@
     gather(out3, extra)
     pack_edges(GRAD0, grad0, 3, False)
     send_halos(GRAD0, grad0, "first")
-    send_all(3, out3, in3, False)
+    send_all(3, out3, in3)
     await_halos(GRAD0, grad0, "first")
     divergence(GRAD0, grad0, spread1)
     pack_edges(SPREAD1, spread1, 1, True)
@@ -452,8 +443,8 @@
 
     out5[...] = summary
 
-    for_others(lambda k, d: pltpu.make_async_remote_copy(
-        src_ref=out5, dst_ref=in5.at[me], send_sem=send_sems.at[5], recv_sem=recv_sems.at[5, 0],
+    for_others(lambda d: pltpu.make_async_remote_copy(
+        src_ref=out5, dst_ref=in5.at[me], send_sem=send_sems.at[5], recv_sem=recv_sems.at[5],
         device_id=d, device_id_type=LOGICAL).start())
     in5[me] = summary
     save_grad.start()
@@ -596,7 +587,7 @@
             pltpu.VMEM((5, 2, nz, LANES), F32),
             pltpu.VMEM((5, 2, nz, LANES), F32),
             pltpu.SemaphoreType.DMA((6,)),
-            pltpu.SemaphoreType.DMA((6, groups)),
+            pltpu.SemaphoreType.DMA((6,)),
             pltpu.SemaphoreType.DMA((6, 4)),
             pltpu.SemaphoreType.DMA((6, 4)),
             pltpu.SemaphoreType.DMA((11,)),

time: 64 us -> 62.8 us (0.981)
  Pallas kernels: 63.2 us -> 62.1 us
    pallas_call x1, Pallas kernels: 58.1 us -> 56.9 us  [shards(): pl.pallas_call(functools.partial(kernel, sizes, torus), name='wind_analys...]
where the time goes in v5:
time: 62.8 us; the launch traced here: 62.7 us
  Pallas kernels  62.1 us (99%)
  between operations  0.64 us (1%)
    pallas_call x1, Pallas kernels, shards(): pl.pallas_call(functools.partial(kernel, sizes, torus), name='wind_analys...  56.9 us
    pallas_call x1, Pallas kernels, shards(): pl.pallas_call(strain_kernel, name='strain', out_shape=(jax.ShapeDtypeStr...  5.13 us

profile of v5, /device:TPU:1, one launch (start us, length us, event | category | flops | bytes accessed | tf_op | source)
XLA Modules:
  0.0 62.7 jit_solution(10814888403784107441)
XLA Ops:
  0.6 56.9 %wind_analysis.1 = (f32[3,18,32,256]{3,2,1,0:T(8,128)}, f32[3,18,32,256]{3,2,1,0:T(8,128)}, f32[5,32,128]{2,1,0:T(8,128)}) custom-call(s32[1,256]{1,0:T(1,128)} %bitcast.3, s32[1,128]{1,0:T(1,128)} %count_hbm.1, f32[3,16,32,256]{3,2,1,0:T(8,128)} %bg_hbm.1, bf16[256,128,128]{2,1,0:T(8,128)(2,1)} %interp_hbm.1, bf16[3,256,128]{2,1,0:T(8,128)(2,1)} %bitcast.2, ...), custom_call_target="tpu_custom_call" | custom-call | tf_op jit(solution)/shard_map/wind_analysis/pallas_call | solution.py:559
  57.6 5.1 %strain.1 = (f32[3,16,32,256]{3,2,1,0:T(8,128)}, f32[6,16,32,256]{3,2,1,0:T(8,128)}, f32[2]{0:T(128)}) custom-call(f32[3,18,32,256]{3,2,1,0:T(8,128)} %get-tuple-element.6.wind_hbm, f32[3,18,32,256]{3,2,1,0:T(8,128)} %get-tuple-element.7.grad_hbm, f32[5,32,128]{2,1,0:T(8,128)} %get-tuple-element.8.info_hbm), custom_call_target="tpu_custom_call" | custom-call | tf_op jit(solution)/shard_map/strain/pallas_call | solution.py:600

commit v6 on v5

--- a/solution.py
+++ b/solution.py
@@ -489,10 +489,10 @@
     diff_y, diff_z = differences(nz, ny)
     load_info = pltpu.make_async_copy(info_hbm, info, info_sem)
     load_info.start()
-    starts = list(range(0, nx + 2, 4))
+    starts = list(range(0, nx + 2, 6))
     loads = []
     for i, start in enumerate(starts):
-        span = pl.ds(start, min(4, nx + 2 - start))
+        span = pl.ds(start, min(6, nx + 2 - start))
         loads.append((
             pltpu.make_async_copy(wind_hbm.at[:, span], wind.at[:, span], wind_sems.at[i]),
             pltpu.make_async_copy(grad_hbm.at[:, span], grad.at[:, span], grad_sems.at[i])))
@@ -511,7 +511,7 @@
         while ready < len(starts) and starts[ready] <= 2 * j + 3:
             for copy in loads[ready]:
                 copy.wait()
-            for x in range(starts[ready], min(starts[ready] + 4, nx + 2)):
+            for x in range(starts[ready], min(starts[ready] + 6, nx + 2)):
                 new = [wind[c, x] - step * grad[c, x] for c in range(3)]
                 for c in range(3):
                     wind[c, x] = new[c]
@@ -596,7 +596,7 @@
             collective_id=0, has_side_effects=True, vmem_limit_bytes=60 * 2**20),
     )(cell_block.reshape(1, n * slots), sweep_count, background, interp, rays, observed)
 
-    spans = len(range(0, nx + 2, 4))
+    spans = len(range(0, nx + 2, 6))
     return pl.pallas_call(
         strain_kernel,
         name="strain",

time: 62.8 us -> 62.6 us (level)
  no operation moved by 1% of the time
where the time goes in v6:
time: 62.6 us; the launch traced here: 62.4 us
  Pallas kernels  61.8 us (99%)
  between operations  0.64 us (1%)
    pallas_call x1, Pallas kernels, shards(): pl.pallas_call(functools.partial(kernel, sizes, torus), name='wind_analys...  56.9 us
    pallas_call x1, Pallas kernels, shards(): pl.pallas_call(strain_kernel, name='strain', out_shape=(jax.ShapeDtypeStr...  4.86 us

profile of v6, /device:TPU:1, one launch (start us, length us, event | category | flops | bytes accessed | tf_op | source)
XLA Modules:
  0.0 62.4 jit_solution(14438234569068430130)
XLA Ops:
  0.6 56.9 %wind_analysis.1 = (f32[3,18,32,256]{3,2,1,0:T(8,128)}, f32[3,18,32,256]{3,2,1,0:T(8,128)}, f32[5,32,128]{2,1,0:T(8,128)}) custom-call(s32[1,256]{1,0:T(1,128)} %bitcast.3, s32[1,128]{1,0:T(1,128)} %count_hbm.1, f32[3,16,32,256]{3,2,1,0:T(8,128)} %bg_hbm.1, bf16[256,128,128]{2,1,0:T(8,128)(2,1)} %interp_hbm.1, bf16[3,256,128]{2,1,0:T(8,128)(2,1)} %bitcast.2, ...), custom_call_target="tpu_custom_call" | custom-call | tf_op jit(solution)/shard_map/wind_analysis/pallas_call | solution.py:559
  57.6 4.9 %strain.1 = (f32[3,16,32,256]{3,2,1,0:T(8,128)}, f32[6,16,32,256]{3,2,1,0:T(8,128)}, f32[2]{0:T(128)}) custom-call(f32[3,18,32,256]{3,2,1,0:T(8,128)} %get-tuple-element.6.wind_hbm, f32[3,18,32,256]{3,2,1,0:T(8,128)} %get-tuple-element.7.grad_hbm, f32[5,32,128]{2,1,0:T(8,128)} %get-tuple-element.8.info_hbm), custom_call_target="tpu_custom_call" | custom-call | tf_op jit(solution)/shard_map/strain/pallas_call | solution.py:600
